TPU v7x, 32 devices: a whole 2x2x4 slice. The times are simulated.
32 devices in a mesh: seq: 4 (over y, x), dp: 8 (over z, core).
Axes of the slice: x: 2, y: 2, z: 4, core: 2. Of those that a mesh axis runs over, the one named last changes fastest.
Arguments:
- frames: bfloat16 [8, 1024, 768], P('dp', 'seq'), may hold values from -6 to 6
- seg_ids: int32 [8, 1024], P('dp'), may hold values from 0 to 2, never falling along the last dimension, each value on 1 to 512 neighbouring positions
- padding: int32 [8, 1024], P('dp'), may hold values from 0 to 1, as said below
- step_ids: int32 [8, 3], P('dp'), may hold values from 0 to 999
- text_states: bfloat16 [8, 3, 256, 1024], P('dp', None, 'seq'), may hold values from -6 to 6
- text_len: int32 [8, 3], P('dp'), may hold values from 77 to 256
- w_ada: bfloat16 [768, 4608], replicated, may hold values from -0.21875 to 0.21875
- w_qkv: bfloat16 [768, 2304], replicated, may hold values from -0.21875 to 0.21875
- w_proj: bfloat16 [768, 768], replicated, may hold values from -1.25 to 1.25
- w_cq: bfloat16 [768, 768], replicated, may hold values from -0.21875 to 0.21875
- w_ckv: bfloat16 [1024, 1536], replicated, may hold values from -0.1875 to 0.1875
- w_cout: bfloat16 [768, 768], replicated, may hold values from -0.875 to 0.875
- w_fc1: bfloat16 [768, 3072], replicated, may hold values from -0.21875 to 0.21875
- w_fc2: bfloat16 [3072, 768], replicated, may hold values from -0.21875 to 0.21875
- cotangent: bfloat16 [8, 1024, 768], P('dp', 'seq'), may hold values from -6 to 6
Outputs:
- block_out: bfloat16 [8, 1024, 768], P('dp', 'seq')
- grad_frames: bfloat16 [8, 1024, 768], P('dp', 'seq')
- grad_text: bfloat16 [8, 3, 256, 1024], P('dp', None, 'seq')
- grad_ada: float32 [768, 4608], P('dp', 'seq')
- grad_qkv: float32 [768, 2304], P('dp', 'seq')
- grad_proj: float32 [768, 768], P('dp', 'seq')
- grad_cq: float32 [768, 768], P('dp', 'seq')
- grad_ckv: float32 [1024, 1536], P('dp', 'seq')
- grad_cout: float32 [768, 768], P('dp', 'seq')
- grad_fc1: float32 [768, 3072], P('dp', 'seq')
- grad_fc2: float32 [3072, 768], P('dp', 'seq')
Inputs may be any that keep to these rules, and one draw needn't show every extreme that they name: `seg_ids`: in every row the clip numbers never fall; each of the 3 clips holds 1 to 512 frames, and one holds exactly 512. In every row the real frames come first, then at most 128 padding frames.
All inputs are finite; a program needn't handle non-finite values.
Results may differ from a plain program's by a relative error of at most 0.022.
Values may be sent and summed in bfloat16 or wider, within the bound.
A program may use at most 192 MiB of HBM per device.

v0:
```python
import math

import jax
import jax.numpy as jnp
from jax import lax
from jax.sharding import PartitionSpec as P

H = 12
HD = 64


highest = lax.Precision.HIGHEST
masked_score = -1e30
epsilon = 1e-06


def embed_steps(step_values, width_all):
    half_width = width_all // 2
    frequency = jnp.exp(
        -math.log(10000.0) * jnp.arange(half_width).astype(jnp.float32) / half_width
    )
    angles = step_values.astype(jnp.float32)[..., None] * frequency
    return jax.nn.silu(jnp.concatenate([jnp.cos(angles), jnp.sin(angles)], axis=-1))


def normalize(values):
    centered = values - jnp.mean(values, axis=-1, keepdims=True)
    return centered * lax.rsqrt(jnp.mean(centered * centered, axis=-1, keepdims=True) + epsilon)


def modulate(values, shift_in, scale_in):
    return normalize(values) * (1.0 + scale_in) + shift_in


def gelu_tanh(values):
    return jax.nn.gelu(values, approximate=True)


def matmul(left, right):
    return jnp.dot(left, right, preferred_element_type=jnp.float32)


def matmul_nt(left, right):
    return jnp.einsum("te,de->td", left, right, preferred_element_type=jnp.float32)


def matmul_tn(left, right):
    return jnp.einsum("td,te->de", left, right, preferred_element_type=jnp.float32)


def self_allowed(seg_block, seg_row, pad_row, start, block_len):
    query_pos = start + jnp.arange(block_len)
    key_pos = jnp.arange(seg_row.shape[1])
    same_clip = seg_block[:, :, None] == seg_row[:, None, :]
    open_key = (pad_row[:, None, :] == 1) | (query_pos[:, None] == key_pos[None, :])[None]
    return same_clip & open_key


def self_scores(query_block, keys, seg_block, seg_row, pad_row, start, block_len, score_scale):
    scores = (
        jnp.einsum("rihe,rjhe->rhij", query_block, keys, preferred_element_type=jnp.float32)
        * score_scale
    )
    allowed = self_allowed(seg_block, seg_row, pad_row, start, block_len)
    return jnp.where(allowed[:, None], scores, masked_score)


def self_forward(query, keys, values, seg_row, pad_row, score_scale):
    row_count, full_len, head_count, head_size = query.shape
    block_len = min(512, full_len)
    block_count = full_len // block_len

    def one_block(index):
        start = index * block_len
        query_block = lax.dynamic_slice_in_dim(query, start, block_len, 1)
        seg_block = lax.dynamic_slice_in_dim(seg_row, start, block_len, 1)
        scores = self_scores(
            query_block, keys, seg_block, seg_row, pad_row, start, block_len, score_scale
        )
        peak = jnp.max(scores, axis=-1, keepdims=True)
        expo = jnp.exp(scores - peak)
        total = jnp.sum(expo, axis=-1, keepdims=True)
        attn_low = (expo / total).astype(jnp.bfloat16)
        output = jnp.einsum("rhij,rjhe->rihe", attn_low, values, preferred_element_type=jnp.float32)
        return (output.astype(jnp.bfloat16), (peak + jnp.log(total))[..., 0])

    outputs, log_totals = lax.map(one_block, jnp.arange(block_count))
    outputs = jnp.moveaxis(outputs, 0, 1).reshape(row_count, full_len, head_count, head_size)
    return (outputs, log_totals)


def self_backward(query, keys, values, grad_out, log_totals, seg_row, pad_row, score_scale):
    row_count, full_len, head_count, head_size = query.shape
    block_len = min(512, full_len)
    block_count = full_len // block_len

    def one_block(carry, inputs):
        d_keys, d_values = carry
        index, lse_block = inputs
        start = index * block_len
        query_block = lax.dynamic_slice_in_dim(query, start, block_len, 1)
        grad_block = lax.dynamic_slice_in_dim(grad_out, start, block_len, 1)
        seg_block = lax.dynamic_slice_in_dim(seg_row, start, block_len, 1)
        scores = self_scores(
            query_block, keys, seg_block, seg_row, pad_row, start, block_len, score_scale
        )
        attn_full = jnp.exp(scores - lse_block[..., None])
        d_attn = jnp.einsum(
            "rihe,rjhe->rhij", grad_block, values, preferred_element_type=jnp.float32
        )
        delta = jnp.sum(attn_full * d_attn, axis=-1, keepdims=True)
        d_scores = (attn_full * (d_attn - delta)).astype(jnp.bfloat16)
        d_query = (
            jnp.einsum("rhij,rjhe->rihe", d_scores, keys, preferred_element_type=jnp.float32)
            * score_scale
        )
        d_keys = (
            d_keys
            + jnp.einsum(
                "rhij,rihe->rjhe", d_scores, query_block, preferred_element_type=jnp.float32
            )
            * score_scale
        )
        d_values = d_values + jnp.einsum(
            "rhij,rihe->rjhe",
            attn_full.astype(jnp.bfloat16),
            grad_block,
            preferred_element_type=jnp.float32,
        )
        return ((d_keys, d_values), d_query.astype(jnp.bfloat16))

    zero_grad = jnp.zeros(keys.shape, jnp.float32)
    (d_keys, d_values), d_query = lax.scan(
        one_block, (zero_grad, zero_grad), (jnp.arange(block_count), log_totals)
    )
    d_query = jnp.moveaxis(d_query, 0, 1).reshape(row_count, full_len, head_count, head_size)
    return (d_query, d_keys.astype(jnp.bfloat16), d_values.astype(jnp.bfloat16))


def cross_allowed(seg_local, text_len, segs_all, text_full):
    key_seg = jnp.repeat(jnp.arange(segs_all), text_full)
    key_pos = jnp.tile(jnp.arange(text_full), segs_all)
    key_len = jnp.sum(
        (key_seg[None, :, None] == jnp.arange(segs_all)[None, None, :]) * text_len[:, None, :],
        axis=-1,
    )
    return (seg_local[:, :, None] == key_seg[None, None, :]) & (key_pos[None, :] < key_len)[
        :, None, :
    ]


def cross_scores(query, keys, allowed, score_scale):
    scores = (
        jnp.einsum("rihe,rjhe->rhij", query, keys, preferred_element_type=jnp.float32) * score_scale
    )
    return jnp.where(allowed[:, None], scores, masked_score)


def cross_forward(query, keys, values, allowed, score_scale):
    scores = cross_scores(query, keys, allowed, score_scale)
    peak = jnp.max(scores, axis=-1, keepdims=True)
    expo = jnp.exp(scores - peak)
    total = jnp.sum(expo, axis=-1, keepdims=True)
    attn_low = (expo / total).astype(jnp.bfloat16)
    output = jnp.einsum("rhij,rjhe->rihe", attn_low, values, preferred_element_type=jnp.float32)
    return (output.astype(jnp.bfloat16), peak + jnp.log(total))


def cross_backward(query, keys, values, grad_out, log_totals, allowed, score_scale):
    scores = cross_scores(query, keys, allowed, score_scale)
    attn_full = jnp.exp(scores - log_totals)
    d_attn = jnp.einsum("rihe,rjhe->rhij", grad_out, values, preferred_element_type=jnp.float32)
    delta = jnp.sum(attn_full * d_attn, axis=-1, keepdims=True)
    d_scores = (attn_full * (d_attn - delta)).astype(jnp.bfloat16)
    d_query = (
        jnp.einsum("rhij,rjhe->rihe", d_scores, keys, preferred_element_type=jnp.float32)
        * score_scale
    )
    d_keys = (
        jnp.einsum("rhij,rihe->rjhe", d_scores, query, preferred_element_type=jnp.float32)
        * score_scale
    )
    d_values = jnp.einsum(
        "rhij,rihe->rjhe",
        attn_full.astype(jnp.bfloat16),
        grad_out,
        preferred_element_type=jnp.float32,
    )
    return (d_query.astype(jnp.bfloat16), d_keys, d_values)


def per_device(
    frames,
    seg_ids,
    padding,
    step_ids,
    text_states,
    text_len,
    w_ada,
    w_qkv,
    w_proj,
    w_cq,
    w_ckv,
    w_cout,
    w_fc1,
    w_fc2,
    cotangent,
):
    row_count, local_len, width_all = frames.shape
    seq_count = lax.axis_size("seq")
    segs_all = step_ids.shape[1]
    full_len = seg_ids.shape[1]
    text_local = text_states.shape[2]
    head_local = H // seq_count
    group_width = head_local * HD
    score_scale = HD ** (-0.5)
    tokens = row_count * local_len
    seq_at = lax.axis_index("seq")
    seg_local = lax.dynamic_slice_in_dim(seg_ids, seq_at * local_len, local_len, 1)
    inputs = frames.astype(jnp.float32).reshape(tokens, width_all)
    emb_low = embed_steps(step_ids, width_all).astype(jnp.bfloat16)
    modulation = jnp.einsum("rsd,de->rse", emb_low, w_ada, preferred_element_type=jnp.float32)
    selector = (seg_local[..., None] == jnp.arange(segs_all)).astype(jnp.float32)
    per_token = jnp.einsum("rls,rse->rle", selector, modulation, precision=highest).reshape(
        tokens, 6 * width_all
    )
    shift_a, scale_a, gate_a, shift_m, scale_m, gate_m = jnp.split(per_token, 6, axis=1)
    normed_a_full, mod_back_a = jax.vjp(modulate, inputs, shift_a, scale_a)
    normed_a = normed_a_full.astype(jnp.bfloat16)

    def project_heads():
        return (
            matmul(normed_a, w_qkv)
            .astype(jnp.bfloat16)
            .reshape(row_count, local_len, 3, seq_count, group_width)
        )

    def split_heads(packed):
        shaped = packed.reshape(row_count, full_len, 3, head_local, HD)
        return (shaped[:, :, 0], shaped[:, :, 1], shaped[:, :, 2])

    head_major = lax.all_to_all(project_heads(), "seq", split_axis=3, concat_axis=1, tiled=True)
    query, keys, values = split_heads(head_major)
    attended, log_totals = self_forward(query, keys, values, seg_ids, padding, score_scale)
    attended = attended.reshape(row_count, full_len, 1, group_width)
    attn_local = lax.all_to_all(attended, "seq", split_axis=1, concat_axis=2, tiled=True).reshape(
        tokens, width_all
    )
    branch_a = matmul(attn_local, w_proj)
    mid_one = inputs + gate_a * branch_a
    normed_c_full, norm_back_c = jax.vjp(normalize, mid_one)
    normed_c = normed_c_full.astype(jnp.bfloat16)
    cross_q = matmul(normed_c, w_cq).astype(jnp.bfloat16).reshape(row_count, local_len, H, HD)
    text_flat = text_states.reshape(-1, text_states.shape[3])
    kv_local = (
        matmul(text_flat, w_ckv)
        .astype(jnp.bfloat16)
        .reshape(row_count, segs_all, text_local, 2 * width_all)
    )
    kv_all = lax.all_gather(kv_local, "seq", axis=2, tiled=True)
    text_full = kv_all.shape[2]
    key_total = segs_all * text_full
    cross_k = kv_all[..., :width_all].reshape(row_count, key_total, H, HD)
    cross_v = kv_all[..., width_all:].reshape(row_count, key_total, H, HD)
    allowed_c = cross_allowed(seg_local, text_len, segs_all, text_full)
    cross_out, cross_lse = cross_forward(cross_q, cross_k, cross_v, allowed_c, score_scale)
    cross_flat = cross_out.reshape(tokens, width_all)
    branch_c = matmul(cross_flat, w_cout)
    mid_two = mid_one + branch_c
    normed_m_full, mod_back_m = jax.vjp(modulate, mid_two, shift_m, scale_m)
    normed_m = normed_m_full.astype(jnp.bfloat16)
    hidden_pre = matmul(normed_m, w_fc1)
    hidden_full, gelu_back = jax.vjp(gelu_tanh, hidden_pre)
    hidden = hidden_full.astype(jnp.bfloat16)
    branch_m = matmul(hidden, w_fc2)
    result = mid_two + gate_m * branch_m
    block_out = result.astype(jnp.bfloat16).reshape(frames.shape)
    grad_y = cotangent.astype(jnp.float32).reshape(tokens, width_all)
    d_branch_m = (gate_m * grad_y).astype(jnp.bfloat16)
    d_gate_m = grad_y * branch_m
    g_fc2 = matmul_tn(hidden, d_branch_m)
    d_hidden = matmul_nt(d_branch_m, w_fc2)
    d_pre = gelu_back(d_hidden)[0].astype(jnp.bfloat16)
    g_fc1 = matmul_tn(normed_m, d_pre)
    d_normed_m = matmul_nt(d_pre, w_fc1)
    d_mid_ln, d_shift_m, d_scale_m = mod_back_m(d_normed_m)
    d_mid_two = grad_y + d_mid_ln
    d_branch_c = d_mid_two.astype(jnp.bfloat16)
    g_cout = matmul_tn(cross_flat, d_branch_c)
    d_cross = (
        matmul_nt(d_branch_c, w_cout).astype(jnp.bfloat16).reshape(row_count, local_len, H, HD)
    )
    d_cross_q, d_cross_k, d_cross_v = cross_backward(
        cross_q, cross_k, cross_v, d_cross, cross_lse, allowed_c, score_scale
    )
    d_kv_part = jnp.concatenate(
        [
            d_cross_k.reshape(row_count, segs_all, text_full, width_all),
            d_cross_v.reshape(row_count, segs_all, text_full, width_all),
        ],
        axis=3,
    )
    d_kv = lax.psum_scatter(
        d_kv_part.astype(jnp.bfloat16), "seq", scatter_dimension=2, tiled=True
    ).reshape(-1, 2 * width_all)
    grad_text = matmul_nt(d_kv, w_ckv).astype(jnp.bfloat16).reshape(text_states.shape)
    g_ckv = matmul_tn(text_flat, d_kv)
    d_cq_flat = d_cross_q.reshape(tokens, width_all)
    g_cq = matmul_tn(normed_c, d_cq_flat)
    d_normed_c = matmul_nt(d_cq_flat, w_cq)
    d_mid_one = d_mid_two + norm_back_c(d_normed_c)[0]
    d_branch_a = (gate_a * d_mid_one).astype(jnp.bfloat16)
    d_gate_a = d_mid_one * branch_a
    g_proj = matmul_tn(attn_local, d_branch_a)
    d_attn_local = (
        matmul_nt(d_branch_a, w_proj)
        .astype(jnp.bfloat16)
        .reshape(row_count, local_len, seq_count, group_width)
    )
    d_heads = lax.all_to_all(d_attn_local, "seq", split_axis=2, concat_axis=1, tiled=True).reshape(
        row_count, full_len, head_local, HD
    )
    query_back, keys_back, values_back = split_heads(
        lax.all_to_all(project_heads(), "seq", split_axis=3, concat_axis=1, tiled=True)
    )
    d_query, d_keys, d_values = self_backward(
        query_back, keys_back, values_back, d_heads, log_totals, seg_ids, padding, score_scale
    )
    d_packed = jnp.stack([d_query, d_keys, d_values], axis=2).reshape(
        row_count, full_len, 3, 1, group_width
    )
    d_qkv = lax.all_to_all(d_packed, "seq", split_axis=1, concat_axis=3, tiled=True).reshape(
        tokens, 3 * width_all
    )
    g_qkv = matmul_tn(normed_a, d_qkv)
    d_normed_a = matmul_nt(d_qkv, w_qkv)
    d_in_ln, d_shift_a, d_scale_a = mod_back_a(d_normed_a)
    grad_frames = (d_mid_one + d_in_ln).astype(jnp.bfloat16).reshape(frames.shape)
    d_per_token = jnp.concatenate(
        [d_shift_a, d_scale_a, d_gate_a, d_shift_m, d_scale_m, d_gate_m], axis=1
    ).reshape(row_count, local_len, 6 * width_all)
    d_modulation = jnp.einsum("rls,rle->rse", selector, d_per_token, precision=highest)
    emb_full = emb_low.astype(jnp.float32)
    g_ada_part = jnp.einsum("rsd,rse->de", emb_full, d_modulation, precision=highest)
    column_parts = (
        lax.psum_scatter(
            g_ada_part.astype(jnp.bfloat16), "seq", scatter_dimension=1, tiled=True
        ).astype(jnp.float32),
        lax.psum_scatter(g_qkv.astype(jnp.bfloat16), "seq", scatter_dimension=1, tiled=True).astype(
            jnp.float32
        ),
        lax.psum_scatter(
            g_proj.astype(jnp.bfloat16), "seq", scatter_dimension=1, tiled=True
        ).astype(jnp.float32),
        lax.psum_scatter(g_cq.astype(jnp.bfloat16), "seq", scatter_dimension=1, tiled=True).astype(
            jnp.float32
        ),
        lax.psum_scatter(g_ckv.astype(jnp.bfloat16), "seq", scatter_dimension=1, tiled=True).astype(
            jnp.float32
        ),
        lax.psum_scatter(
            g_cout.astype(jnp.bfloat16), "seq", scatter_dimension=1, tiled=True
        ).astype(jnp.float32),
        lax.psum_scatter(g_fc1.astype(jnp.bfloat16), "seq", scatter_dimension=1, tiled=True).astype(
            jnp.float32
        ),
        lax.psum_scatter(g_fc2.astype(jnp.bfloat16), "seq", scatter_dimension=1, tiled=True).astype(
            jnp.float32
        ),
    )
    sharded = (
        lax.psum_scatter(column_parts[0], "dp", scatter_dimension=0, tiled=True),
        lax.psum_scatter(column_parts[1], "dp", scatter_dimension=0, tiled=True),
        lax.psum_scatter(column_parts[2], "dp", scatter_dimension=0, tiled=True),
        lax.psum_scatter(column_parts[3], "dp", scatter_dimension=0, tiled=True),
        lax.psum_scatter(column_parts[4], "dp", scatter_dimension=0, tiled=True),
        lax.psum_scatter(column_parts[5], "dp", scatter_dimension=0, tiled=True),
        lax.psum_scatter(column_parts[6], "dp", scatter_dimension=0, tiled=True),
        lax.psum_scatter(column_parts[7], "dp", scatter_dimension=0, tiled=True),
    )
    grad_ada = sharded[0]
    rest = sharded[1:]
    return (
        block_out,
        grad_frames,
        grad_text,
        grad_ada,
        rest[0],
        rest[1],
        rest[2],
        rest[3],
        rest[4],
        rest[5],
        rest[6],
    )


def solution(mesh):
    return jax.shard_map(
        per_device,
        mesh=mesh,
        in_specs=(
            P("dp", "seq", None),
            P("dp", None),
            P("dp", None),
            P("dp", None),
            P("dp", None, "seq", None),
            P("dp", None),
            P(),
            P(),
            P(),
            P(),
            P(),
            P(),
            P(),
            P(),
            P("dp", "seq", None),
        ),
        out_specs=(
            P("dp", "seq", None),
            P("dp", "seq", None),
            P("dp", None, "seq", None),
            P("dp", "seq"),
            P("dp", "seq"),
            P("dp", "seq"),
            P("dp", "seq"),
            P("dp", "seq"),
            P("dp", "seq"),
            P("dp", "seq"),
            P("dp", "seq"),
        ),
        check_vma=False,
    )
```

profile of v0, /device:TPU:0, one launch (start us, length us, event | category | flops | bytes accessed | tf_op | source)
XLA Modules:
  0.0 1016.8 jit_solution(9007225352317419361)
XLA Ops:
  28.2 5.2 all-to-all-start
  37.3 11.8 %all-to-all-done = bf16[1,256,3,4,192]{1,4,2,0,3:T(8,128)(2,1)} async-done(((bf16[1,256,3,4,192]{1,4,2,0,3:T(8,128)(2,1)}), bf16[1,256,3,4,192]{1,4,2,0,3:T(8,128)(2,1)}, u32[]{:S(2)}, u32[]{:S(2)}) %all-to-all-start) | async-done | bytes 1179680 | tf_op jit(solution)/shard_map/all_to_all | solution.py:242
  59.3 21.1 %while.27 = (s32[]{:T(128)}, bf16[2,1,512,3,64]{2,4,3,1,0:T(8,128)(2,1)}, f32[2,1,3,512]{3,2,1,0:T(4,128)}, s32[2]{0:T(128)}, s32[1,1024]{1,0:T(1,128)S(1)}, /*i...) while((s32[]{:T(128)}, ...), condition=%wide.region_5.6_spmd, body=%wide.region_2.5_spmd.sunk | while | flops 423723008 | bytes 27048288 | solution.py:87
  88.6 5.7 reduce.18
  133.0 4.1 reshape.936
  172.6 6.4 fusion.69
  179.0 7.9 multiply_reduce_fusion.1
  190.6 7.4 multiply_convert_fusion.1
  205.9 6.9 pad_maximum_fusion
  212.8 7.3 copy.168
  222.1 85.5 %all-reduce.3.cloned.1.call-done = bf16[1,3,256,1536]{3,1,0,2:T(4,128)(2,1)} async-done(((bf16[1,3,256,1536]{3,1,0,2:T(4,128)(2,1)}), bf16[1,3,256,1536]{3,1,0,2:T(4,128)(2,1)}) %all-reduce.3.cloned.1.call-update) | async-done | bytes 2359312
  315.5 4.4 fusion.74
  338.0 4.6 all-to-all-done.2
  347.4 28.5 %while.28 = (s32[]{:T(128)}, f32[1,1024,3,64]{1,3,2,0:T(8,128)}, f32[1,1024,3,64]{1,3,2,0:T(8,128)}, bf16[2,1,512,3,64]{2,4,3,1,0:T(8,128)(2,1)}, s32[2]{0:T(128...) while((s32[]{:T(128)}, f32[1,1024,3,64]{1,3,2,0:T(8,128)}, ...), condition=%wide.region_20.21_spmd.clone, body=%wide.region_18.20_spmd.clone.sunk | while | flops 1033502720 | bytes 76679712 | solution.py:133
  388.7 36.3 %all_to_all.65 = bf16[1,1024,3,1,192]{4,2,3,0,1:T(4,128)(2,1)} all-to-all(bf16[1,1024,3,1,192]{4,2,3,0,1:T(4,128)(2,1)} %copy.165), channel_id=1, replica_groups=mesh['seq'=4,'dp'=8] {'seq'}, dimensions={1} | all-to-all | bytes 2359296 | tf_op jit(solution)/shard_map/all_to_all | solution.py:332
  425.0 4.3 copy.176
  436.0 5.9 convolution_convert_fusion.2
  442.0 5.3 convolution_convert_fusion.3
  456.3 7.8 convolution_convert_fusion
  464.1 10.3 %copy.177 = bf16[768,4608]{0,1:T(8,128)(2,1)} copy(bf16[768,4608]{1,0:T(8,128)(2,1)} %convolution_convert_fusion) | data formatting | bytes 14155776
  483.6 32.0 %reduce-scatter.29.cloned.1.call-done = bf16[768,576]{0,1:T(8,128)(2,1)} async-done(((bf16[768,2304]{0,1:T(8,128)(2,1)}), bf16[768,576]{0,1:T(8,128)(2,1)}) %reduce-scatter.29.cloned.1.call-update) | async-done | bytes 884752 | tf_op jit(solution)/shard_map/reduce_scatter | solution.py:349
  518.2 57.4 %reduce-scatter.45.cloned.1.call-done = bf16[3072,192]{0,1:T(8,128)(2,1)} async-done(((bf16[3072,768]{0,1:T(8,128)(2,1)}), bf16[3072,192]{0,1:T(8,128)(2,1)}) %reduce-scatter.45.cloned.1.call-update) | async-done | bytes 1179664 | tf_op jit(solution)/shard_map/reduce_scatter | solution.py:367
  578.6 56.9 %reduce-scatter.41.cloned.1.call-done = bf16[768,768]{1,0:T(8,128)(2,1)} async-done(((bf16[768,3072]{1,0:T(8,128)(2,1)}), bf16[768,768]{1,0:T(8,128)(2,1)}) %reduce-scatter.41.cloned.1.call-update) | async-done | bytes 1179664 | tf_op jit(solution)/shard_map/reduce_scatter | solution.py:364
  638.4 76.6 %reduce-scatter.49.cloned.1.call-done = bf16[1152,768]{1,0:T(8,128)(2,1)} async-done(((bf16[4608,768]{1,0:T(8,128)(2,1)}), bf16[1152,768]{1,0:T(8,128)(2,1)}) %reduce-scatter.49.cloned.1.call-update) | async-done | bytes 1769488
  727.8 23.9 %reduce-scatter.37.cloned.1.call-done = f32[128,384]{0,1:T(8,128)} async-done(((f32[1024,384]{0,1:T(8,128)}), f32[128,384]{0,1:T(8,128)}) %reduce-scatter.37.cloned.1.call-update) | async-done | bytes 196624 | tf_op jit(solution)/shard_map/reduce_scatter | solution.py:376
  753.5 31.0 %reduce-scatter.57.cloned.1.call-done = f32[96,192]{1,0:T(8,128)} async-done(((f32[768,192]{1,0:T(8,128)}), f32[96,192]{1,0:T(8,128)}) %reduce-scatter.57.cloned.1.call-update) | async-done | bytes 73744
  784.5 33.1 %reduce-scatter.53.cloned.1.call-done = f32[96,192]{1,0:T(8,128)} async-done(((f32[768,192]{1,0:T(8,128)}), f32[96,192]{1,0:T(8,128)}) %reduce-scatter.53.cloned.1.call-update) | async-done | bytes 73744
  817.5 33.0 %reduce-scatter.55.cloned.1.call-done = f32[96,192]{1,0:T(8,128)} async-done(((f32[768,192]{1,0:T(8,128)}), f32[96,192]{1,0:T(8,128)}) %reduce-scatter.55.cloned.1.call-update) | async-done | bytes 73744
  850.6 37.1 %reduce-scatter.51.cloned.1.call-done = f32[96,576]{1,0:T(8,128)} async-done(((f32[768,576]{1,0:T(8,128)}), f32[96,576]{1,0:T(8,128)}) %reduce-scatter.51.cloned.1.call-update) | async-done | bytes 221200
  887.7 38.0 %reduce-scatter.47.cloned.1.call-done = f32[384,192]{0,1:T(8,128)} async-done(((f32[3072,192]{0,1:T(8,128)}), f32[384,192]{0,1:T(8,128)}) %reduce-scatter.47.cloned.1.call-update) | async-done | bytes 294928 | tf_op jit(solution)/shard_map/reduce_scatter | solution.py:379
  925.6 38.7 %reduce-scatter.43.cloned.1.call-done = f32[96,768]{1,0:T(8,128)} async-done(((f32[768,768]{1,0:T(8,128)}), f32[96,768]{1,0:T(8,128)}) %reduce-scatter.43.cloned.1.call-update) | async-done | bytes 294928 | tf_op jit(solution)/shard_map/reduce_scatter | solution.py:378
  964.4 45.4 %reduce-scatter.27.cloned.1.call-done = f32[96,1152]{1,0:T(8,128)} async-done(((f32[768,1152]{1,0:T(8,128)}), f32[96,1152]{1,0:T(8,128)}) %reduce-scatter.27.cloned.1.call-update) | async-done | bytes 442384 | tf_op jit(solution)/shard_map/reduce_scatter | solution.py:372
  (405 shorter events, 267.3 us)
Async XLA Ops:
  7.2 14.2 %copy-start = (bf16[768,2304]{1,0:T(8,128)(2,1)S(1)}, bf16[768,2304]{1,0:T(8,128)(2,1)}, u32[]{:S(2)}) copy-start(bf16[768,2304]{1,0:T(8,128)(2,1)} %param.26) | copy-start | bytes 10616836
  9.3 8.8 copy-start.57
  11.2 6.9 copy-start.75
  28.2 20.9 %all-to-all-start = ((bf16[1,256,3,4,192]{1,4,2,0,3:T(8,128)(2,1)}), bf16[1,256,3,4,192]{1,4,2,0,3:T(8,128)(2,1)}, u32[]{:S(2)}, u32[]{:S(2)}) async-start(bf16[1,256,3,4,192]{1,4,2,0,3:T(8,128)(2,1)} %copy.151), calls=%async_computation | async-start | bytes 2359296 | tf_op jit(solution)/shard_map/all_to_all | solution.py:242
  33.4 92.7 %all-gather.2.cloned.1.call-start = ((), (), s32[]{:S(2)}) async-start(), calls=%async_computation.20 | async-start | bytes 2949120 | tf_op jit(solution)/shard_map/all_gather | solution.py:260
  52.3 7.0 copy-start.50
  52.3 7.0 copy-start.53
  96.7 10.4 %all-to-all-start.1 = ((bf16[4,2,24576]{2,1,0:T(2,128)(2,1)}), bf16[4,2,24576]{2,1,0:T(2,128)(2,1)}, u32[]{:S(2)}, u32[]{:S(2)}) async-start(bf16[4,2,24576]{2,1,0:T(2,128)(2,1)} %reshape.972), calls=%async_computation.1 | async-start | bytes 786432 | tf_op jit(solution)/shard_map/all_to_all | solution.py:246
  100.8 206.8 %all-reduce.3.cloned.1.call-start = ((), (), s32[]{:S(2)}) async-start(), calls=%async_computation.37 | async-start | bytes 6291456
  148.1 8.9 slice-start
  150.0 8.0 slice-start.4
  156.7 9.6 copy-start.11
  157.0 9.3 copy-start.63
  172.6 6.4 copy-start.54
  190.6 9.6 copy-start.28
  220.2 254.3 %reduce-scatter.35.cloned.1.call-start = ((), (), s32[]{:S(2)}) async-start(), calls=%async_computation.25 | async-start | bytes 3932160 | tf_op jit(solution)/shard_map/reduce_scatter | solution.py:358
  312.7 164.5 %reduce-scatter.39.cloned.1.call-start = ((), (), s32[]{:S(2)}) async-start(), calls=%async_computation.27 | async-start | bytes 1474560 | tf_op jit(solution)/shard_map/reduce_scatter | solution.py:361
  315.4 163.9 %reduce-scatter.31.cloned.1.call-start = ((), (), s32[]{:S(2)}) async-start(), calls=%async_computation.23 | async-start | bytes 1474560 | tf_op jit(solution)/shard_map/reduce_scatter | solution.py:352
  330.5 12.1 %all-to-all-start.2 = ((bf16[1,256,4,192]{1,3,0,2:T(8,128)(2,1)}), bf16[1,256,4,192]{1,3,0,2:T(8,128)(2,1)}, u32[]{:S(2)}, u32[]{:S(2)}) async-start(bf16[1,256,4,192]{1,3,0,2:T(8,128)(2,1)} %bitcast.338), calls=%async_computation.2 | async-start | bytes 786432 | tf_op jit(solution)/shard_map/all_to_all | solution.py:320
  334.6 146.9 %reduce-scatter.33.cloned.1.call-start = ((), (), s32[]{:S(2)}) async-start(), calls=%async_computation.24 | async-start | bytes 1474560 | tf_op jit(solution)/shard_map/reduce_scatter | solution.py:355
  337.6 178.0 %reduce-scatter.29.cloned.1.call-start = ((), (), s32[]{:S(2)}) async-start(), calls=%async_computation.22 | async-start | bytes 4423680 | tf_op jit(solution)/shard_map/reduce_scatter | solution.py:349
  435.7 139.8 %reduce-scatter.45.cloned.1.call-start = ((), (), s32[]{:S(2)}) async-start(), calls=%async_computation.30 | async-start | bytes 5898240 | tf_op jit(solution)/shard_map/reduce_scatter | solution.py:367
  441.9 193.6 %reduce-scatter.41.cloned.1.call-start = ((), (), s32[]{:S(2)}) async-start(), calls=%async_computation.28 | async-start | bytes 5898240 | tf_op jit(solution)/shard_map/reduce_scatter | solution.py:364
  447.3 267.8 %reduce-scatter.49.cloned.1.call-start = ((), (), s32[]{:S(2)}) async-start(), calls=%async_computation.32 | async-start | bytes 8847360
  474.4 277.3 %reduce-scatter.37.cloned.1.call-start = ((), (), s32[]{:S(2)}) async-start(), calls=%async_computation.26 | async-start | bytes 1769472 | tf_op jit(solution)/shard_map/reduce_scatter | solution.py:376
  477.2 307.3 %reduce-scatter.57.cloned.1.call-start = ((), (), s32[]{:S(2)}) async-start(), calls=%async_computation.36 | async-start | bytes 884736
  479.3 338.2 %reduce-scatter.53.cloned.1.call-start = ((), (), s32[]{:S(2)}) async-start(), calls=%async_computation.34 | async-start | bytes 884736
  481.4 369.1 %reduce-scatter.55.cloned.1.call-start = ((), (), s32[]{:S(2)}) async-start(), calls=%async_computation.35 | async-start | bytes 884736
  483.5 404.1 %reduce-scatter.51.cloned.1.call-start = ((), (), s32[]{:S(2)}) async-start(), calls=%async_computation.33 | async-start | bytes 2211840
  518.1 407.5 %reduce-scatter.47.cloned.1.call-start = ((), (), s32[]{:S(2)}) async-start(), calls=%async_computation.31 | async-start | bytes 2654208 | tf_op jit(solution)/shard_map/reduce_scatter | solution.py:379
  578.6 385.8 %reduce-scatter.43.cloned.1.call-start = ((), (), s32[]{:S(2)}) async-start(), calls=%async_computation.29 | async-start | bytes 2654208 | tf_op jit(solution)/shard_map/reduce_scatter | solution.py:378
  638.4 371.4 %reduce-scatter.27.cloned.1.call-start = ((), (), s32[]{:S(2)}) async-start(), calls=%async_computation.21 | async-start | bytes 3981312 | tf_op jit(solution)/shard_map/reduce_scatter | solution.py:372
  (88 other events, 190.6 us)
Sparse Core Ops, SparseCore 0:
  37.4 39.6 all-gather.1
  220.3 87.2 all-reduce.2
  312.8 46.2 reduce-scatter.34
  361.9 28.7 reduce-scatter.38
  393.4 40.2 reduce-scatter.30
  436.5 28.7 reduce-scatter.32
  468.4 47.1 reduce-scatter.28
  518.5 56.9 reduce-scatter.44
  578.5 56.9 reduce-scatter.40
  638.4 76.5 reduce-scatter.48
  717.3 34.3 reduce-scatter.36
  754.4 29.9 reduce-scatter.56
  787.3 30.1 reduce-scatter.52
  820.2 30.2 reduce-scatter.54
  853.3 34.3 reduce-scatter.50
  890.4 35.1 reduce-scatter.46
  928.4 35.9 reduce-scatter.42
  967.1 42.5 reduce-scatter.26
where the time goes:
time: 1020 us
  waiting for transfers between devices  609 us (60%)
  local copies, waits for them, and re-layouts  149 us (15%)
  matrix products  125 us (12%)
  other arithmetic  62.9 us (6%)
  blocking collectives  36.3 us (4%)
  between operations  16.1 us (2%)
  starting transfers between devices  14.9 us (1%)
    unnamed x24, waiting for transfers between devices  297 us
    reduce_scatter x1, waiting for transfers between devices, per_device(): lax.psum_scatter(g_fc2.astype(jnp.bfloat16), 'seq', scatter_dimension=1,...  57.4 us
    reduce_scatter x1, waiting for transfers between devices, per_device(): lax.psum_scatter(g_fc1.astype(jnp.bfloat16), 'seq', scatter_dimension=1,...  56.9 us
    unnamed x151, local copies, waits for them, and re-layouts  49.6 us
    reduce_scatter x1, waiting for transfers between devices, per_device(): lax.psum_scatter(column_parts[0], 'dp', scatter_dimension=0, tiled=True)  45.4 us
    reduce_scatter x1, waiting for transfers between devices, per_device(): lax.psum_scatter(column_parts[6], 'dp', scatter_dimension=0, tiled=True)  38.7 us
    reduce_scatter x1, waiting for transfers between devices, per_device(): lax.psum_scatter(column_parts[7], 'dp', scatter_dimension=0, tiled=True)  38 us
    all_to_all x1, blocking collectives, per_device(): lax.all_to_all(d_packed, 'seq', split_axis=1, concat_axis=3, tiled=True)  36.3 us
  transfers between devices with their start and end apart: 21, of which 16 were waited for; matrix products, arithmetic and copies ran while one was open for 20% of the time, Pallas kernels for 0%

commit v1 on v0

v1 whole, which is shorter than its diff:
```python
import functools
import math

import jax
import jax.numpy as jnp
from jax import lax
from jax.experimental import pallas as pl
from jax.experimental.pallas import tpu as pltpu
from jax.sharding import PartitionSpec as P

H = 12
HD = 64
BLOCKS = 8
SEQ = "seq"
DP = "dp"
CUT, COLS, PACK = 3, 1, 2
BF = jnp.bfloat16
F32 = jnp.float32
MESH = pl.DeviceIdType.MESH
MASKED = -1e30
EPS = 1e-06
SCALE = HD ** (-0.5)
ANY = pl.BlockSpec(memory_space=pl.ANY)
INV = pl.BlockSpec(memory_space=pltpu.VMEM)


def nn(a, b):
    return lax.dot_general(a, b, (((1,), (0,)), ((), ())), preferred_element_type=F32)


def nt(a, b):
    return lax.dot_general(a, b, (((1,), (1,)), ((), ())), preferred_element_type=F32)


def tn(a, b):
    return lax.dot_general(a, b, (((0,), (0,)), ((), ())), preferred_element_type=F32)


def embed_steps(step_values, width_all):
    half_width = width_all // 2
    frequency = jnp.exp(
        -math.log(10000.0) * jnp.arange(half_width).astype(F32) / half_width
    )
    angles = step_values.astype(F32)[..., None] * frequency
    return jax.nn.silu(jnp.concatenate([jnp.cos(angles), jnp.sin(angles)], axis=-1))


def norm_parts(v):
    centered = v - jnp.mean(v, axis=-1, keepdims=True)
    rstd = lax.rsqrt(jnp.mean(centered * centered, axis=-1, keepdims=True) + EPS)
    return centered * rstd, rstd


def norm_back(g, n, rstd):
    return (g - jnp.mean(g, axis=-1, keepdims=True) - n * jnp.mean(g * n, axis=-1, keepdims=True)) * rstd


def pick(mods, seg, part, width):
    low = part * width
    a = mods[0:1, low : low + width]
    b = mods[1:2, low : low + width]
    c = mods[2:3, low : low + width]
    return jnp.where(seg == 0.0, a, jnp.where(seg == 1.0, b, c))


def column(row):
    return jnp.broadcast_to(row, (128, row.shape[1])).T


class Bag(dict):
    __getattr__ = dict.__getitem__


class Remote:
    def __init__(self, send, recv):
        self.send, self.recv, self.used, self.open = send, recv, 0, []

    def slots(self, count):
        first = self.used
        self.used += count
        return first

    def make(self, src, dst, slot, where):
        return pltpu.make_async_remote_copy(
            src_ref=src,
            dst_ref=dst,
            send_sem=self.send.at[slot],
            recv_sem=self.recv.at[slot],
            device_id=where,
            device_id_type=MESH,
        )

    def start(self, describe):
        slot = self.slots(1)

        def again():
            src, dst, where = describe()
            return self.make(src, dst, slot, where)

        again().start()
        self.open.append(again)
        return again


class Local:
    def __init__(self, sems):
        self.sems, self.used = sems, 0

    def start(self, src, dst):
        copy = pltpu.make_async_copy(src, dst, self.sems.at[self.used])
        self.used += 1
        copy.start()
        return copy


def greet(seq, at_seq, dp_peers):
    barrier = pltpu.get_barrier_semaphore()
    for k in range(1, seq):
        pl.semaphore_signal(
            barrier, inc=1, device_id={SEQ: lax.rem(at_seq + k, seq)}, device_id_type=MESH
        )
    for peer in dp_peers:
        pl.semaphore_signal(barrier, inc=1, device_id={DP: peer}, device_id_type=MESH)
    pl.semaphore_wait(barrier, seq - 1 + len(dp_peers))


K1_OUTS = tuple(dict(h1=0, qT=0, kT=0, kn=0, vn=0, lse=0, oT=0, aout=0, x1=0, h2T=0, cqT=0, kv=0, ckT=0, lsec=0, coT=0, x2=0, text=0))


def forward_kernel(dims, *refs):
    seq, tok, full, width, keys, group, dc = dims
    hl = H // seq
    ins, refs = refs[:9], refs[9:]
    x_hbm, text_hbm, codes, mods, wg_hbm, wckv_hbm, wp_hbm, wcq_hbm, wco_hbm = ins
    outs, refs = Bag(zip(K1_OUTS, refs[: len(K1_OUTS)])), refs[len(K1_OUTS) :]
    (
        x_all, text_all, wg, wckv, wp, wcq, wco, qT, kT, vT, kn, vn, lse, osend, orecv, aout, x1, h2T, cqT, kv, kvT,
        lsec, coT, x2, bias, biasc, kcol, tcol, xin, lsem, ssem, rsem,
    ) = refs
    local, remote = Local(lsem), Remote(ssem, rsem)
    s = lax.axis_index(SEQ)
    load_x = local.start(x_hbm, xin)
    load_own = local.start(x_hbm, x_all.at[s])
    load_wg = local.start(wg_hbm, wg)
    load_text = local.start(text_hbm, text_all.at[s])
    load_w = [local.start(a, b) for a, b in ((wckv_hbm, wckv), (wp_hbm, wp), (wcq_hbm, wcq), (wco_hbm, wco))]
    greet(seq, s, ())

    base_x = remote.slots(seq)
    base_t = remote.slots(seq)
    base_o = remote.slots(seq)

    def send_x(k):
        return remote.make(x_hbm, x_all.at[s], base_x + k, {SEQ: lax.rem(s + k, seq)})

    def send_t(k):
        return remote.make(text_hbm, text_all.at[s], base_t + k, {SEQ: lax.rem(s + k, seq)})

    for k in range(1, seq):
        send_x(k).start()
    for k in range(1, seq):
        send_t(k).start()

    kcol[...] = column(codes[1:2, :full])
    tcol[...] = column(codes[2:3, :keys])
    load_x.wait()
    load_own.wait()
    load_wg.wait()

    def project(k, carry):
        @pl.when(k > 0)
        def _():
            send_x(k).wait_recv()

        at = lax.rem(s - k + seq, seq)
        rows = pl.ds(pl.multiple_of(at * tok, tok), tok)
        seg = column(codes[0:1, rows])[:, :1]
        seg = jnp.broadcast_to(seg, (tok, width))
        n, _ = norm_parts(x_all[at].astype(F32))
        h1 = (n * (1.0 + pick(mods, seg, 1, width)) + pick(mods, seg, 0, width)).astype(BF)
        x_all[at] = h1
        out = nn(h1, wg[...])
        for h in range(hl):
            kn[h, rows, :] = out[:, group + h * HD : group + (h + 1) * HD].astype(BF)
            vn[h, rows, :] = out[:, 2 * group + h * HD : 2 * group + (h + 1) * HD].astype(BF)
        low = out.astype(BF).astype(F32)
        outT = low.T
        qT[:, rows] = (outT[:group] * SCALE).astype(BF)
        kT[:, rows] = outT[group : 2 * group].astype(BF)
        vT[:, rows] = outT[2 * group :].astype(BF)
        return carry

    lax.fori_loop(0, seq, project, 0)
    saves = [
        local.start(a, b)
        for a, b in ((x_all, outs.h1), (qT, outs.qT), (kT, outs.kT), (kn, outs.kn), (vn, outs.vn))
    ]

    def send_o(k):
        at = lax.rem(s + k, seq)
        return remote.make(osend.at[at], orecv.at[s], base_o + k, {SEQ: at})

    def attend(k, carry):
        at = lax.rem(s + 1 + k, seq)
        rows = pl.ds(pl.multiple_of(at * tok, tok), tok)
        seg = codes[0:1, rows]
        row_id = lax.broadcasted_iota(jnp.int32, (full, tok), 0)
        col_id = lax.broadcasted_iota(jnp.int32, (full, tok), 1) + at * tok
        key = jnp.broadcast_to(kcol[:, :1], (full, tok))
        bias[...] = jnp.where((key == seg) | (row_id == col_id), 0.0, MASKED)

        def head(h, c2):
            hrows = pl.ds(pl.multiple_of(h * HD, HD), HD)
            st = nn(kn[h], qT[hrows, rows]) + bias[...]
            peak = jnp.max(st, axis=0, keepdims=True)
            ex = jnp.exp(st - peak)
            total = jnp.sum(ex, axis=0, keepdims=True)
            ov = nn(vT[hrows, :], ex.astype(BF)) * (1.0 / total)
            osend[at, hrows, :] = ov.astype(BF)
            lse[pl.ds(h, 1), rows] = peak + jnp.log(total)
            return c2

        lax.fori_loop(0, hl, head, 0)

        @pl.when(k < seq - 1)
        def _():
            send_o(k + 1).start()

        return carry

    lax.fori_loop(0, seq, attend, 0)
    orecv[s] = osend[s]

    load_text.wait()
    for k in range(1, seq):
        send_t(k).wait_recv()
    saves.append(local.start(text_all, outs.text))
    saves.append(local.start(lse, outs.lse))
    for c in load_w:
        c.wait()
    tl = keys // seq

    def project_text(b, carry):
        trows = pl.ds(pl.multiple_of(b * tl, tl), tl)
        kv[trows, :] = nn(text_all[b], wckv[...]).astype(BF)
        return carry

    lax.fori_loop(0, seq, project_text, 0)

    def turn_text(c, carry):
        cols = pl.ds(pl.multiple_of(c * 256, 256), 256)
        kvT[cols, :] = kv[:, cols].astype(F32).T.astype(BF)
        return carry

    lax.fori_loop(0, 2 * width // 256, turn_text, 0)
    rows = pl.ds(pl.multiple_of(s * tok, tok), tok)
    seg_row = codes[0:1, rows]
    biasc[...] = jnp.where(jnp.broadcast_to(tcol[:, :1], (keys, tok)) == seg_row, 0.0, MASKED)
    saves.append(local.start(kv, outs.kv))
    saves.append(local.start(kvT.at[pl.ds(0, width)], outs.ckT))

    for k in range(1, seq):
        send_o(k).wait_recv()
    saves.append(local.start(orecv, outs.oT))
    seg = jnp.broadcast_to(column(seg_row)[:, :1], (tok, width))
    branch = tn(orecv[...].reshape(width, tok), wp[...])
    aout[...] = branch
    mid = xin[...].astype(F32) + pick(mods, seg, 2, width) * branch
    x1[...] = mid
    n, _ = norm_parts(mid)
    h2 = n.astype(BF)
    h2T[...] = n.astype(BF).astype(F32).T.astype(BF)
    cq = nn(h2, wcq[...]).astype(BF).astype(F32)
    cqT[...] = (cq.T * SCALE).astype(BF)
    saves += [local.start(a, b) for a, b in ((aout, outs.aout), (x1, outs.x1), (h2T, outs.h2T), (cqT, outs.cqT))]

    def cross(p, carry):
        cols = pl.ds(pl.multiple_of(p * 128, 128), 128)
        pair = kv[:, cols]
        for a in range(2):
            hrows = pl.ds(pl.multiple_of(p * 128 + a * HD, HD), HD)
            vrows = pl.ds(pl.multiple_of(width + p * 128 + a * HD, HD), HD)
            st = nn(pair[:, a * HD : (a + 1) * HD], cqT[hrows, :]) + biasc[...]
            peak = jnp.max(st, axis=0, keepdims=True)
            ex = jnp.exp(st - peak)
            total = jnp.sum(ex, axis=0, keepdims=True)
            ov = nn(kvT[vrows, :], ex.astype(BF)) * (1.0 / total)
            coT[hrows, :] = ov.astype(BF)
            lsec[pl.ds(2 * p + a, 1), :] = peak + jnp.log(total)
        return carry

    lax.fori_loop(0, H // 2, cross, 0)
    x2[...] = x1[...] + tn(coT[...], wco[...])
    saves += [local.start(a, b) for a, b in ((lsec, outs.lsec), (coT, outs.coT), (x2, outs.x2))]
    for k in range(1, seq):
        send_x(k).wait_send()
        send_t(k).wait_send()
        send_o(k).wait_send()
    for c in saves:
        c.wait()


def run_forward(dims, args):
    seq, tok, full, width, keys, group, dc = dims
    hl = H // seq
    shapes = dict(
        h1=((seq, tok, width), BF),
        qT=((group, full), BF),
        kT=((group, full), BF),
        kn=((hl, full, HD), BF),
        vn=((hl, full, HD), BF),
        lse=((8, full), F32),
        oT=((seq, group, tok), BF),
        aout=((tok, width), F32),
        x1=((tok, width), F32),
        h2T=((width, tok), BF),
        cqT=((width, tok), BF),
        kv=((keys, 2 * width), BF),
        ckT=((width, keys), BF),
        lsec=((16, tok), F32),
        coT=((width, tok), BF),
        x2=((tok, width), F32),
        text=((seq, keys // seq, dc), BF),
    )
    v = pltpu.VMEM
    scratch = [
        v((seq, tok, width), BF), v((seq, keys // seq, dc), BF), v((width, 3 * group), BF), v((dc, 2 * width), BF),
        v((width, width), BF), v((width, width), BF), v((width, width), BF),
        v((group, full), BF), v((group, full), BF), v((group, full), BF), v((hl, full, HD), BF), v((hl, full, HD), BF),
        v((8, full), F32), v((seq, group, tok), BF), v((seq, group, tok), BF),
        v((tok, width), F32), v((tok, width), F32), v((width, tok), BF), v((width, tok), BF),
        v((keys, 2 * width), BF), v((2 * width, keys), BF), v((16, tok), F32), v((width, tok), BF), v((tok, width), F32),
        v((full, tok), F32), v((keys, tok), F32), v((full, 128), F32), v((keys, 128), F32), v((tok, width), BF),
        pltpu.SemaphoreType.DMA((32,)), pltpu.SemaphoreType.DMA((3 * seq,)), pltpu.SemaphoreType.DMA((3 * seq,)),
    ]
    outs = pl.pallas_call(
        functools.partial(forward_kernel, dims),
        out_shape=[jax.ShapeDtypeStruct(*shapes[n]) for n in K1_OUTS],
        in_specs=[ANY, ANY, INV, INV, ANY, ANY, ANY, ANY, ANY],
        out_specs=[ANY] * len(K1_OUTS),
        scratch_shapes=scratch,
        compiler_params=pltpu.CompilerParams(
            collective_id=0, has_side_effects=True, vmem_limit_bytes=60 * 1024 * 1024
        ),
        name="forward_part",
    )(*args)
    return Bag(zip(K1_OUTS, outs))


class Grad:
    def __init__(self, ref, kind, order, bufs, where, remote, finish):
        self.ref, self.kind, self.order, self.bufs = ref, kind, order, bufs
        self.s, self.seq, self.d, self.stride, self.bits = where
        self.remote, self.finish = remote, finish
        self.fixed, self.cut, self.stage, self.copies = {}, False, 0, []

    def view(self, fixed, quarter, lead=None):
        index, lead = [], list(lead or [])
        for bit in (2, 1, 0):
            if bit in fixed:
                index.append(fixed[bit])
            elif lead:
                index.append(lead.pop(0))
            else:
                index.append(slice(None))
        if quarter is not None:
            size = self.ref.shape[-1] // (self.seq if self.kind == COLS else 2)
            if self.kind == COLS:
                lanes = pl.ds(pl.multiple_of(quarter * size, 128), size)
                index += [slice(None), lanes]
            else:
                lanes = pl.ds(pl.multiple_of(lax.rem(quarter, 2) * size, 128), size)
                index += [lax.div(quarter, 2), slice(None), lanes]
        return self.ref.at[tuple(index)]

    def begin(self):
        what, buf = self.order[self.stage], self.bufs[self.stage]
        self.copies = []
        if what == CUT:
            for k in range(1, self.seq):

                def describe(k=k, fixed=dict(self.fixed)):
                    to = lax.rem(self.s + k, self.seq)
                    return self.view(fixed, to), buf.at[k - 1], {SEQ: to}

                self.copies.append(self.remote.start(describe))
        else:

            def describe(fixed=dict(self.fixed), quarter=self.s if self.cut else None):
                mine = self.bits[what]
                peer = self.d + (1 - 2 * mine) * (self.stride << what)
                return self.view({**fixed, what: 1 - mine}, quarter), buf, {DP: peer}

            self.copies.append(self.remote.start(describe))

    def end(self):
        what, buf = self.order[self.stage], self.bufs[self.stage]
        for c in self.copies:
            c().wait_recv()
        if what == CUT:
            self.cut = True
        else:
            self.fixed[what] = self.bits[what]
        free = 3 - len(self.fixed)
        quarter = self.s if self.cut else None
        last = self.stage == len(self.order) - 1
        self.stage += 1

        def add(i, carry):
            lead = [lax.rem(lax.div(i, 2 ** (free - 1 - j)), 2) for j in range(free)]
            own = self.view(self.fixed, quarter, lead)
            total = own[...].astype(F32)
            if what == CUT:
                for k in range(self.seq - 1):
                    total = total + buf[tuple([k] + lead)].astype(F32)
            elif lead:
                total = total + buf[tuple(lead)].astype(F32)
            else:
                total = total + buf[...].astype(F32)
            if last:
                self.finish(total)
            else:
                own[...] = total.astype(BF)
            return carry

        if free == 0:
            add(0, 0)
        else:
            lax.fori_loop(0, 2**free, add, 0)

    def step(self):
        self.end()
        if self.stage < len(self.order):
            self.begin()


def grad_buffers(shape, kind, order, seq):
    lead, payload, out, cut, free = 3, list(shape), [], False, 3
    for what in order:
        if what == CUT:
            cut = True
        else:
            free -= 1
        p = list(payload)
        if cut:
            if kind == COLS:
                p[-1] //= seq
            else:
                p = [p[1], p[2] // 2]
        head = [seq - 1] if what == CUT else []
        out.append(pltpu.VMEM(tuple(head + [2] * free + p), BF))
    return out


GRADS = dict(
    fc2=(PACK, (0, CUT, 1, 2)),
    fc1=(COLS, (0, 1, 2, CUT)),
    cout=(PACK, (0, CUT, 1, 2)),
    cq=(PACK, (0, CUT, 1, 2)),
    proj=(PACK, (0, CUT, 1, 2)),
    ckv=(None, (0, 1, 2)),
    qkv=(None, (0, 1, 2)),
)
K2_OUTS = tuple(dict(block_out=0, grad_frames=0, grad_text=0, ada=0, qkv=0, proj=0, cq=0, ckv=0, cout=0, fc1=0, fc2=0))
K2_LOADS = tuple(dict(x2=0, x1=0, aout=0, oT=0, h2T=0, cqT=0, coT=0, lsec=0, lse=0, kv=0))
K2_HELD = tuple(dict(ckT=0, qT=0, kT=0, kn=0, vn=0))
K2_WEIGHTS = tuple(dict(fc1=0, fc2=0, cout=0, cq=0, proj=0))


def backward_kernel(dims, names, dp, *refs):
    seq, tok, full, width, keys, group, dc_all = dims
    hl, chunk, tl, stride = H // seq, width, keys // seq, dp // BLOCKS
    r = Bag(zip(names, refs))
    local, remote = Local(r.lsem), Remote(r.ssem, r.rsem)
    s, d = lax.axis_index(SEQ), lax.axis_index(DP)
    bits = [lax.rem(lax.div(d, stride << b), 2) for b in range(3)]
    where = (s, seq, d, stride, bits)
    codes, mods = r.codes, r.mods

    loads = Bag()
    loads["x2"] = local.start(r.in_x2, r.x2)
    loads["cot"] = local.start(r.in_cot, r.cot)
    for n in K2_WEIGHTS:
        loads["w_" + n] = local.start(r["w_" + n], r["g_" + n])
    for n in K2_LOADS[1:]:
        loads[n] = local.start(r["in_" + n], r[n])
    loads.x = local.start(r.in_x, r.x)

    barrier = pltpu.get_barrier_semaphore()
    for k in range(1, seq):
        pl.semaphore_signal(barrier, inc=1, device_id={SEQ: lax.rem(s + k, seq)}, device_id_type=MESH)

    def greet_dp(j, carry):
        pl.semaphore_signal(barrier, inc=1, device_id={DP: lax.rem(d + j, dp)}, device_id_type=MESH)
        return carry

    lax.fori_loop(1, dp, greet_dp, 0)
    pl.semaphore_wait(barrier, seq - 1 + dp - 1)

    emb_base = remote.slots(dp)
    dm_base = remote.slots(dp)

    def send_emb(j):
        to = lax.rem(d + j, dp)
        return remote.make(r.in_emb.at[to], r.emball.at[d], emb_base + j, {DP: to})

    def start_emb(j, carry):
        send_emb(j).start()
        return carry

    lax.fori_loop(1, dp, start_emb, 0)
    own_emb = local.start(r.in_emb.at[d], r.emball.at[d])

    def into_cols(n):
        def finish(total):
            r["out_" + n][...] = total

        return finish

    def into_pack(n):
        def finish(total):
            rows, lanes = total.shape
            r["out_" + n][0:rows, :] = total[:, : lanes // 2]
            r["out_" + n][rows : 2 * rows, :] = total[:, lanes // 2 :]

        return finish

    def into_blocks(total):
        for t in range(3):
            r.fq[t] = total[:, t * group : (t + 1) * group]

    grads = Bag()
    for n, (kind, order) in GRADS.items():
        finish = into_blocks if n == "qkv" else (into_pack(n) if kind == PACK else into_cols(n))
        bufs = [r["r_%s%d" % (n, i)] for i in range(len(order))]
        grads[n] = Grad(r["g_" + n], kind, order, bufs, where, remote, finish)

    rows_own = pl.ds(pl.multiple_of(s * tok, tok), tok)
    seg_row = codes[0:1, rows_own]
    seg = jnp.broadcast_to(column(seg_row)[:, :1], (tok, width))
    clip_id = lax.broadcasted_iota(jnp.int32, (16, tok), 0).astype(F32)
    onehot = jnp.where(clip_id == seg_row, 1.0, 0.0).astype(BF)

    def clip_sum(part, value):
        high = value.astype(BF)
        rest = (value - high.astype(F32)).astype(BF)
        r.dmod[:, part * width : (part + 1) * width] = (nn(onehot, high) + nn(onehot, rest))[:8]

    def square(n, lhs, rhs):
        g = r["g_" + n]

        def four(i, carry):
            val = nn(lhs(i), rhs).astype(BF)
            for g0 in range(2):
                for q in range(seq):
                    half = val.shape[0] // 4
                    low = g0 * 2 * half
                    lane = (q % 2) * 2 * group
                    at = (lax.div(i, 2), lax.rem(i, 2), g0, q // 2)
                    g[at + (slice(None), slice(lane, lane + group))] = val[low : low + half, q * group : (q + 1) * group]
                    g[at + (slice(None), slice(lane + group, lane + 2 * group))] = val[
                        low + half : low + 2 * half, q * group : (q + 1) * group
                    ]
            return carry

        lax.fori_loop(0, 4, four, 0)

    def weight(n):
        return r["g_" + n][...].reshape(width, width)

    v = pltpu.VMEM
    dkv_copies = []
    quarter = 2 * width // seq
    do_base = remote.slots(seq)

    def send_do(k):
        to = lax.rem(s + k, seq)
        return remote.make(r.dosend.at[to], r.dorecv.at[s], do_base + k, {SEQ: to})

    def middle(*held):
        for n, ref in zip(K2_HELD, held):
            r[n] = ref
            loads[n] = local.start(r["in_" + n], ref)

        loads.x2.wait()
        loads.cot.wait()
        x2v = r.x2[...]
        n3, _ = norm_parts(x2v)
        h3 = (n3 * (1.0 + pick(mods, seg, 4, width)) + pick(mods, seg, 3, width)).astype(BF)

        def feed(h3_ref, h3T_ref, dm_ref, m_ref, dh_ref):
            h3_ref[...] = h3
            h3T_ref[...] = h3.astype(F32).T.astype(BF)
            dm_ref[...] = (pick(mods, seg, 5, width) * r.cot[...].astype(F32)).astype(BF)
            m_ref[...] = jnp.zeros_like(m_ref)
            dh_ref[...] = jnp.zeros_like(dh_ref)
            loads.w_fc1.wait()
            loads.w_fc2.wait()
            g1, g2 = r.g_fc1, r.g_fc2
            k0, k1 = math.sqrt(2.0 / math.pi), 0.044715

            def one(c, carry):
                cols = pl.ds(pl.multiple_of(c * chunk, chunk), chunk)
                ca, cb = lax.div(c, 2), lax.rem(c, 2)
                w1 = g1[:, :, :, :, cols].reshape(width, chunk)
                w2 = g2[ca, cb].reshape(chunk, width)
                z = nn(h3_ref[...], w1)
                zz = z * z
                t = jnp.tanh(k0 * (z + k1 * z * zz))
                u = (0.5 * z * (1.0 + t)).astype(BF)
                slope = 0.5 * (1.0 + t) + 0.5 * z * (1.0 - t * t) * (k0 * (1.0 + 3.0 * k1 * zz))
                m_ref[...] += nn(u, w2)
                dz = (nt(dm_ref[...], w2) * slope).astype(BF)
                dh_ref[...] += nt(dz, w1)
                g1[:, :, :, :, cols] = nn(h3T_ref[...], dz).astype(BF).reshape(2, 2, 2, width // BLOCKS, chunk)
                for g0 in range(2):
                    half = chunk // 4
                    val = tn(u[:, g0 * 2 * half : (g0 + 1) * 2 * half], dm_ref[...]).astype(BF)
                    for q in range(seq):
                        lane = (q % 2) * 2 * group
                        g2[ca, cb, g0, q // 2, :, lane : lane + group] = val[:half, q * group : (q + 1) * group]
                        g2[ca, cb, g0, q // 2, :, lane + group : lane + 2 * group] = val[half:, q * group : (q + 1) * group]
                return carry

            lax.fori_loop(0, seq, one, 0)
            grads.fc2.begin()
            grads.fc1.begin()
            dy = r.cot[...].astype(F32)
            m = m_ref[...]
            x2w = r.x2[...]
            r.out_block_out[...] = (x2w + pick(mods, seg, 5, width) * m).astype(BF)
            clip_sum(5, dy * m)
            dh = dh_ref[...]
            nw, rstd = norm_parts(x2w)
            clip_sum(3, dh)
            clip_sum(4, dh * nw)
            r.dx[...] = dy + norm_back(dh * (1.0 + pick(mods, seg, 4, width)), nw, rstd)

        pl.run_scoped(feed, v((tok, width), BF), v((width, tok), BF), v((tok, width), BF), v((tok, width), F32), v((tok, width), F32))

        for c in (loads.w_cout, loads.coT, loads.cqT, loads.lsec, loads.kv, loads.ckT):
            c.wait()

        def cross_back(dcoT, dcqT, biasc):
            dc = r.dx[...].astype(BF)
            dcoT[...] = nt(weight("cout"), dc).astype(BF)
            square("cout", lambda i: r.coT[pl.ds(pl.multiple_of(i * group, group), group), :], dc)
            grads.cout.begin()
            tcol = column(codes[2:3, :keys])
            biasc[...] = jnp.where(jnp.broadcast_to(tcol[:, :1], (keys, tok)) == seg_row, 0.0, MASKED)
            grads.fc2.step()
            grads.fc1.step()
            kv = r.kv

            def pair(p, carry):
                cols = pl.ds(pl.multiple_of(p * 128, 128), 128)
                vcols = pl.ds(pl.multiple_of(width + p * 128, 128), 128)
                ck, cv = kv[:, cols], kv[:, vcols]
                parts_k, parts_v = [], []
                for a in range(2):
                    hrows = pl.ds(pl.multiple_of(p * 128 + a * HD, HD), HD)
                    q_h, do_h = r.cqT[hrows, :], dcoT[hrows, :]
                    lse_h = r.lsec[pl.ds(2 * p + a, 1), :]
                    pr = jnp.exp(nn(ck[:, a * HD : (a + 1) * HD], q_h) + biasc[...] - lse_h)
                    dpr = nn(cv[:, a * HD : (a + 1) * HD], do_h)
                    delta = jnp.sum(pr * dpr, axis=0, keepdims=True)
                    ds = (pr * (dpr - delta)).astype(BF)
                    parts_k.append(nt(ds, q_h))
                    parts_v.append(nt(pr.astype(BF), do_h))
                    dcqT[hrows, :] = nn(r.ckT[hrows, :], ds) * SCALE
                kv[:, cols] = jnp.concatenate(parts_k, axis=1).astype(BF)
                kv[:, vcols] = jnp.concatenate(parts_v, axis=1).astype(BF)
                return carry

            lax.fori_loop(0, H // 2, pair, 0)
            dcq = dcqT[...].T.astype(BF)
            loads.w_cq.wait()
            loads.h2T.wait()
            loads.x1.wait()
            dh2 = nt(dcq, weight("cq"))
            square("cq", lambda i: r.h2T[pl.ds(pl.multiple_of(i * group, group), group), :], dcq)
            nw, rstd = norm_parts(r.x1[...])
            r.dx[...] += norm_back(dh2, nw, rstd)

        pl.run_scoped(cross_back, v((width, tok), BF), v((width, tok), F32), v((keys, tok), F32))

        for c in (loads.w_proj, loads.aout, loads.oT):
            c.wait()
        dx1 = r.dx[...]
        da = (pick(mods, seg, 2, width) * dx1).astype(BF)
        doT = nt(weight("proj"), da).astype(BF)
        for q in range(seq):
            r.dosend[q] = doT[q * group : (q + 1) * group, :]
        for k in range(1, seq):
            send_do(k).start()
        r.dorecv[s] = r.dosend[s]
        grads.cq.begin()
        clip_sum(2, dx1 * r.aout[...])
        square("proj", lambda i: r.oT[i], da)
        grads.proj.begin()
        grads.cout.step()
        grads.fc1.step()
        for k in range(1, seq):

            def describe_kv(k=k):
                to = lax.rem(s + k, seq)
                lanes = pl.ds(pl.multiple_of(to * quarter, quarter), quarter)
                return r.kv.at[:, lanes], r.dkvr.at[k - 1], {SEQ: to}

            dkv_copies.append(remote.start(describe_kv))
        grads.fc2.step()
        for c in (loads.qT, loads.kT, loads.kn, loads.vn, loads.lse):
            c.wait()

        def self_back(kcol, bias, dk, dv):
            kcol[...] = column(codes[1:2, :full])
            dk[...] = jnp.zeros_like(dk)
            dv[...] = jnp.zeros_like(dv)

            def block(k, carry):
                @pl.when(k > 0)
                def _():
                    send_do(k).wait_recv()

                at = lax.rem(s - k + seq, seq)
                rows = pl.ds(pl.multiple_of(at * tok, tok), tok)
                row_id = lax.broadcasted_iota(jnp.int32, (full, tok), 0)
                col_id = lax.broadcasted_iota(jnp.int32, (full, tok), 1) + at * tok
                key = jnp.broadcast_to(kcol[:, :1], (full, tok))
                bias[...] = jnp.where((key == codes[0:1, rows]) | (row_id == col_id), 0.0, MASKED)
                for h in range(hl):
                    hs = slice(h * HD, (h + 1) * HD)
                    q_h, do_h = r.qT[hs, rows], r.dorecv[at, hs, :]
                    pr = jnp.exp(nn(r.kn[h], q_h) + bias[...] - r.lse[h : h + 1, rows])
                    dpr = nn(r.vn[h], do_h)
                    delta = jnp.sum(pr * dpr, axis=0, keepdims=True)
                    ds = (pr * (dpr - delta)).astype(BF)
                    dk[h] += nt(ds, q_h)
                    dv[h] += nt(pr.astype(BF), do_h)
                    dq = nn(r.kT[hs, :], ds) * SCALE
                    r.dqs[at, :, hs] = dq.T.astype(BF)
                return carry

            lax.fori_loop(0, seq, block, 0)
            for h in range(hl):
                for b in range(seq):
                    br = slice(b * tok, (b + 1) * tok)
                    r.dqs[b, :, group + h * HD : group + (h + 1) * HD] = dk[h, br, :].astype(BF)
                    r.dqs[b, :, 2 * group + h * HD : 2 * group + (h + 1) * HD] = dv[h, br, :].astype(BF)

        pl.run_scoped(self_back, v((full, 128), F32), v((full, tok), F32), v((hl, full, HD), F32), v((hl, full, HD), F32))

    pl.run_scoped(
        middle,
        v((width, keys), BF),
        v((group, full), BF),
        v((group, full), BF),
        v((hl, full, HD), BF),
        v((hl, full, HD), BF),
    )

    dq_base = remote.slots(seq)

    def send_dq(k):
        to = lax.rem(s + k, seq)
        return remote.make(r.dqs.at[to], r.dqr.at[s], dq_base + k, {SEQ: to})

    for k in range(1, seq):
        send_dq(k).start()
    r.dqr[s] = r.dqs[s]

    def tail(h1, text, wqkv, wckv, dqf):
        tail_loads = [
            local.start(a, b)
            for a, b in ((r.in_h1, h1), (r.w_qkv, wqkv), (r.in_text, text), (r.w_ckv, wckv))
        ]
        loads.x.wait()
        tail_loads[0].wait()
        gq = tn(h1[...].reshape(full, width), r.dqs[...].reshape(full, 3 * group))
        r.g_qkv[...] = gq.astype(BF).reshape(2, 2, 2, width // BLOCKS, 3 * group)
        grads.qkv.begin()
        grads.cq.step()
        grads.proj.step()
        grads.fc2.step()
        grads.cout.step()
        grads.fc1.step()
        for c in dkv_copies:
            c().wait_recv()
        own = r.kv[:, pl.ds(pl.multiple_of(s * quarter, quarter), quarter)].astype(F32)
        for k in range(seq - 1):
            own = own + r.dkvr[k].astype(F32)
        r.dkvq[...] = own.astype(BF).reshape(seq, tl, quarter)
        kv_base = remote.slots(seq)

        def send_kv(k):
            to = lax.rem(s + k, seq)
            return remote.make(r.dkvq.at[to], r.dkvl.at[s], kv_base + k, {SEQ: to})

        for k in range(1, seq):
            send_kv(k).start()
        r.dkvl[s] = r.dkvq[s]
        tail_loads[2].wait()
        gc = tn(text[...].reshape(keys, dc_all), r.dkvq[...].reshape(keys, quarter))
        r.g_ckv[...] = gc.astype(BF).reshape(2, 2, 2, dc_all // BLOCKS, quarter)
        grads.ckv.begin()
        grads.qkv.step()
        for k in range(1, seq):
            send_dq(k).wait_recv()
        for b in range(seq):
            got = r.dqr[b]
            for t in range(3):
                dqf[:, t * width + b * group : t * width + (b + 1) * group] = got[:, t * group : (t + 1) * group]
        tail_loads[1].wait()
        dh1 = nt(dqf[...], wqkv[...])
        nx, rstd = norm_parts(r.x[...].astype(F32))
        clip_sum(0, dh1)
        clip_sum(1, dh1 * nx)
        dm_copies = []
        part = 6 * width // seq
        for k in range(1, seq):

            def describe_dm(k=k):
                to = lax.rem(s + k, seq)
                lanes = pl.ds(pl.multiple_of(to * part, part), part)
                return r.dmod.at[:, lanes], r.dmr.at[k - 1], {SEQ: to}

            dm_copies.append(remote.start(describe_dm))
        back = norm_back(dh1 * (1.0 + pick(mods, seg, 1, width)), nx, rstd)
        r.out_grad_frames[...] = (r.dx[...] + back).astype(BF)
        grads.ckv.step()
        grads.qkv.step()
        grads.cq.step()
        grads.proj.step()
        for c in dm_copies:
            c().wait_recv()
        total = r.dmod[:, pl.ds(pl.multiple_of(s * part, part), part)]
        for k in range(seq - 1):
            total = total + r.dmr[k]
        r.dmall[d] = total

        def send_dm(j):
            to = lax.rem(d + j, dp)
            return remote.make(r.dmall.at[d], r.dmall.at[d], dm_base + j, {DP: to})

        def start_dm(j, carry):
            send_dm(j).start()
            return carry

        lax.fori_loop(1, dp, start_dm, 0)
        for k in range(1, seq):
            send_kv(k).wait_recv()
        tail_loads[3].wait()
        gt = nt(r.dkvl[0], wckv[:, 0:quarter])
        for b in range(1, seq):
            gt = gt + nt(r.dkvl[b], wckv[:, b * quarter : (b + 1) * quarter])
        r.out_grad_text[...] = gt.astype(BF)
        grads.fc2.step()
        grads.cout.step()
        grads.qkv.step()
        q_base = remote.slots(3)

        def send_q(t):
            b = 4 * t + s
            to = lax.div(b, 3)
            slot = b - 3 * to
            return to, slot, pltpu.make_async_remote_copy(
                src_ref=r.fq.at[t],
                dst_ref=r.rq.at[slot],
                send_sem=r.ssem.at[q_base + t],
                recv_sem=r.rsem.at[q_base + slot],
                device_id={SEQ: to},
                device_id_type=MESH,
            )

        for t in range(3):
            to, slot, copy = send_q(t)

            @pl.when(to != s)
            def _():
                copy.start()

            @pl.when(to == s)
            def _():
                r.rq[slot] = r.fq[t]

        grads.ckv.step()
        grads.cq.step()
        grads.proj.step()
        grads.fc1.step()
        grads.cout.step()
        grads.ckv.step()
        grads.cq.step()
        grads.proj.step()

        def wait_dm(j, carry):
            send_dm(j).wait_recv()
            send_emb(j).wait_recv()
            return carry

        own_emb.wait()
        lax.fori_loop(1, dp, wait_dm, 0)
        emb = r.emball[...].reshape(dp * 8, 128)
        allm = r.dmall[...].reshape(dp * 8, part)
        high = allm.astype(BF)
        rest = (allm - high.astype(F32)).astype(BF)
        ga = tn(emb, high) + tn(emb, rest)
        r.out_ada[...] = ga[: width // dp]
        for j in range(3):
            src = lax.rem(3 * s + j, seq)

            @pl.when(src != s)
            def _():
                remote.make(r.fq.at[j], r.rq.at[j], q_base + j, {SEQ: src}).wait_recv()

            r.out_qkv[:, j * group : (j + 1) * group] = r.rq[j]

        for t in range(3):
            to, slot, copy = send_q(t)

            @pl.when(to != s)
            def _():
                copy.wait_send()

        for k in range(1, seq):
            send_do(k).wait_send()
            send_dq(k).wait_send()
            send_kv(k).wait_send()

        def wait_sent(j, carry):
            send_dm(j).wait_send()
            send_emb(j).wait_send()
            return carry

        lax.fori_loop(1, dp, wait_sent, 0)
        for c in remote.open:
            c().wait_send()

    pl.run_scoped(
        tail,
        v((seq, tok, width), BF),
        v((seq, tl, dc_all), BF),
        v((width, 3 * width), BF),
        v((dc_all, 2 * width), BF),
        v((tok, 3 * width), BF),
    )


def run_backward(dims, dp, fwd, args):
    seq, tok, full, width, keys, group, dc = dims
    hl, tl, block = H // seq, keys // seq, width // BLOCKS
    ff = 4 * width
    v = pltpu.VMEM
    lead = (2, 2, 2)
    gshape = dict(
        fc1=(block, ff),
        fc2=(2, ff // BLOCKS // 2, width),
        cout=(2, block // 2, width),
        cq=(2, block // 2, width),
        proj=(2, block // 2, width),
        ckv=(dc // BLOCKS, 2 * width // seq),
        qkv=(block, 3 * group),
    )
    names, ins, specs = [], [], []

    def add_in(spec=ANY, **kw):
        for name, value in kw.items():
            names.append(name)
            ins.append(value)
            specs.append(spec)

    add_in(codes=args.codes, spec=INV)
    add_in(mods=args.mods, spec=INV)
    add_in(in_x=args.x)
    add_in(in_cot=args.cot)
    add_in(in_emb=args.emb)
    for n in K2_LOADS + K2_HELD + ("h1", "text"):
        add_in(**{"in_" + n: fwd[n]})
    for n in K2_WEIGHTS:
        add_in(**{"w_" + n: args[n].reshape(lead + gshape[n])})
    add_in(w_ckv=args.ckv)
    add_in(w_qkv=args.qkv)

    outs = dict(
        block_out=((tok, width), BF),
        grad_frames=((tok, width), BF),
        grad_text=((tl, dc), BF),
        ada=((width // dp, 6 * width // seq), F32),
        qkv=((block, 3 * group), F32),
        proj=((block, group), F32),
        cq=((block, group), F32),
        ckv=((dc // BLOCKS, 2 * width // seq), F32),
        cout=((block, group), F32),
        fc1=((block, ff // seq), F32),
        fc2=((ff // BLOCKS, group), F32),
    )
    for n in K2_OUTS:
        names.append("out_" + n)
    scratch = []

    def add(**kw):
        for name, (shape, dtype) in kw.items():
            names.append(name)
            scratch.append(v(shape, dtype))

    add(cot=((tok, width), BF))
    add(x=((tok, width), BF))
    for n in K2_LOADS:
        add(**{n: (fwd[n].shape, fwd[n].dtype)})
    for n, (kind, order) in GRADS.items():
        add(**{"g_" + n: (lead + gshape[n], BF)})
        for i, b in enumerate(grad_buffers(gshape[n], kind, order, seq)):
            names.append("r_%s%d" % (n, i))
            scratch.append(b)
    quarter = 2 * width // seq
    add(dx=((tok, width), F32))
    add(dkvr=((seq - 1, keys, quarter), BF))
    add(dkvq=((seq, tl, quarter), BF))
    add(dkvl=((seq, tl, quarter), BF))
    add(dosend=((seq, group, tok), BF))
    add(dorecv=((seq, group, tok), BF))
    add(dqs=((seq, tok, 3 * group), BF))
    add(dqr=((seq, tok, 3 * group), BF))
    add(dmod=((8, 6 * width), F32))
    add(dmr=((seq - 1, 8, 6 * width // seq), F32))
    add(dmall=((dp, 8, 6 * width // seq), F32))
    add(emball=((dp, 8, 128), BF))
    add(fq=((3, block, group), F32))
    add(rq=((3, block, group), F32))
    count = 2 * dp + 64
    for n, k in dict(lsem=40, ssem=count, rsem=count).items():
        names.append(n)
        scratch.append(pltpu.SemaphoreType.DMA((k,)))
    got = pl.pallas_call(
        functools.partial(backward_kernel, dims, tuple(names), dp),
        out_shape=[jax.ShapeDtypeStruct(*outs[n]) for n in K2_OUTS],
        in_specs=specs,
        out_specs=[INV] * len(K2_OUTS),
        scratch_shapes=scratch,
        compiler_params=pltpu.CompilerParams(
            collective_id=1, has_side_effects=True, vmem_limit_bytes=67043328
        ),
        name="backward_part",
    )(*ins)
    return Bag(zip(K2_OUTS, got))


def per_device(
    frames, seg_ids, padding, step_ids, text_states, text_len, w_ada, w_qkv, w_proj, w_cq, w_ckv, w_cout, w_fc1, w_fc2,
    cotangent,
):
    rows, tok, width = frames.shape
    seq, dp = lax.axis_size(SEQ), lax.axis_size(DP)
    segs = step_ids.shape[1]
    full = seg_ids.shape[1]
    tl, dc = text_states.shape[2], text_states.shape[3]
    keys = segs * tl * seq
    group = (H // seq) * HD
    dims = (seq, tok, full, width, keys, group, dc)
    s = lax.axis_index(SEQ)

    emb = embed_steps(step_ids[0], width).astype(BF)
    mods = jnp.dot(emb, w_ada, preferred_element_type=F32)
    mods = jnp.pad(mods, ((0, 8 - segs), (0, 0)))
    span = width // dp
    emb_parts = jnp.pad(
        jnp.swapaxes(emb.reshape(segs, dp, span), 0, 1), ((0, 0), (0, 8 - segs), (0, 128 - span))
    )
    place = jnp.arange(keys)
    clip = (place // tl) % segs
    position = (place // (tl * segs)) * tl + place % tl
    length = jnp.sum(jnp.where(clip[None, :] == jnp.arange(segs)[:, None], text_len[0][:, None], 0), axis=0)
    text_code = jnp.where(position < length, clip, -1)
    codes = jnp.stack(
        [seg_ids[0], jnp.where(padding[0] == 1, seg_ids[0], -1), jnp.pad(text_code, (0, full - keys))]
    ).astype(F32)
    codes = jnp.pad(codes, ((0, 5), (0, 0)))
    x = frames[0]
    text = text_states.reshape(segs * tl, dc)
    w_group = lax.dynamic_index_in_dim(
        w_qkv.reshape(width, 3, seq, group), s, 2, keepdims=False
    ).reshape(width, 3 * group)
    fwd = run_forward(dims, (x, text, codes, mods, w_group, w_ckv, w_proj, w_cq, w_cout))
    args = Bag(
        codes=codes, mods=mods, x=x, cot=cotangent[0], emb=emb_parts, ckv=w_ckv, qkv=w_qkv,
        fc1=w_fc1, fc2=w_fc2, cout=w_cout, cq=w_cq, proj=w_proj,
    )
    g = run_backward(dims, dp, fwd, args)
    stride = dp // BLOCKS
    if stride > 1:
        groups = [[b * stride + j for j in range(stride)] for b in range(BLOCKS)]
        for n in GRADS:
            g[n] = lax.psum_scatter(g[n], DP, scatter_dimension=0, axis_index_groups=groups, tiled=True)
    return (
        g.block_out.reshape(frames.shape),
        g.grad_frames.reshape(frames.shape),
        g.grad_text.reshape(text_states.shape),
        g.ada, g.qkv, g.proj, g.cq, g.ckv, g.cout, g.fc1, g.fc2,
    )


def solution(mesh):
    own, row, rep = P(DP, SEQ, None), P(DP, None), P()
    text, grad = P(DP, None, SEQ, None), P(DP, SEQ)
    return jax.shard_map(
        per_device,
        mesh=mesh,
        in_specs=(own, row, row, row, text, row) + (rep,) * 8 + (own,),
        out_specs=(own, own, text) + (grad,) * 8,
        check_vma=False,
    )
```

time: 1020 us -> 232 us (0.23)
  waiting for transfers between devices: 609 us -> 0 us
  Pallas kernels: 0 us -> 203 us
  local copies, waits for them, and re-layouts: 149 us -> 21.1 us
  matrix products: 125 us -> 4.17 us
  other arithmetic: 62.9 us -> 3.15 us
  blocking collectives: 36.3 us -> 0 us
  between operations: 16.1 us -> 0.76 us
  starting transfers between devices: 14.9 us -> 0 us
    unnamed x24 -> x0, waiting for transfers between devices: 297 us -> none
    reduce_scatter x11 -> x0, waiting for transfers between devices: 292 us -> none  [the longest x1 57.4 us: per_device(): lax.psum_scatter(g_fc2.astype(jnp.bfloat16), 'seq', scatter_dimension=1,...]
    pallas_call x0 -> x2, Pallas kernels: none -> 203 us  [the longest x1 147 us: run_backward(): pl.pallas_call(functools.partial(backward_kernel, dims, tuple(names), dp)...]
    dot_general x45 -> x1, matrix products: 125 us -> 4.17 us  [per_device(): mods = jnp.dot(emb, w_ada, preferred_element_type=F32)]
    all_to_all x1 -> x0, blocking collectives: 36.3 us -> none  [per_device(): lax.all_to_all(d_packed, 'seq', split_axis=1, concat_axis=3, tiled=True)]
    unnamed x151 -> x26, local copies, waits for them, and re-layouts: 49.6 us -> 16.6 us
    convert_element_type x13 -> x2, other arithmetic: 28.4 us -> 1.36 us  [the longest x1 0.71 us: per_device(): codes = jnp.stack([seg_ids[0], jnp.where(padding[0] == 1, seg_ids[0], -1)...]
    another operation x11 -> x0, local copies, waits for them, and re-layouts: 22.8 us -> none
  transfers between devices with their start and end apart: 21 -> 0, of which waited for: 16 -> 0; matrix products, arithmetic and copies ran while one was open for 20% -> 0% of each run, Pallas kernels for 0% -> 0%
where the time goes in v1:
time: 232 us
  Pallas kernels  203 us (88%)
  local copies, waits for them, and re-layouts  21.1 us (9%)
  matrix products  4.17 us (2%)
  other arithmetic  3.15 us (1%)
    pallas_call x1, Pallas kernels, run_backward(): pl.pallas_call(functools.partial(backward_kernel, dims, tuple(names), dp)...  147 us
    pallas_call x1, Pallas kernels, run_forward(): pl.pallas_call(functools.partial(forward_kernel, dims), out_shape=[jax.Sh...  55.6 us
    unnamed x26, local copies, waits for them, and re-layouts  16.6 us

profile of v1, /device:TPU:0, one launch (start us, length us, event | category | flops | bytes accessed | tf_op | source)
XLA Modules:
  0.0 231.8 jit_solution(8932423969824110064)
XLA Ops:
  0.6 0.7 convert_bitcast_fusion
  1.3 0.7 compare_select_fusion
  2.1 0.7 select_reduce_fusion
  2.8 0.7 add_convert_fusion
  3.5 0.1 multiply_cosine_fusion.1
  3.7 0.1 multiply_cosine_fusion
  3.8 0.6 pad.19.refs_4_
  4.5 0.6 pad.17.refs_2_.refs_0_
  5.1 4.2 %fusion.7 = f32[3,4608]{1,0:T(4,128)S(1)} fusion(bf16[768,4608]{1,0:T(8,128)(2,1)} %param.21, f32[3,384]{1,0:T(4,128)S(1)} %get-tuple-element.114, f32[3,384]{1,0:T(4,128)S(1)} %get-tuple-element.113), kind=kOutput, calls=%fused_computation.23 | convolution fusion | flops 21247488 | bytes 7142400 | tf_op jit(solution)/shard_map/dot_general | solution.py:1062
  9.2 0.7 pad.18.refs_3_.refs_1_
  9.9 0.0 copy-done
  9.9 3.6 %copy.36 = bf16[768,2304]{0,1:T(8,128)(2,1)} copy(bf16[768,2304]{1,0:T(8,128)(2,1)S(1)} %copy-done) | data formatting | bytes 7077888 | tf_op args[7]
  13.5 1.2 constant_dynamic-slice_fusion
  14.7 1.3 copy.37.refs_4_
  16.0 55.6 %forward_part.1 = (bf16[4,256,768]{2,1,0:T(8,128)(2,1)}, bf16[192,1024]{1,0:T(8,128)(2,1)}, bf16[192,1024]{1,0:T(8,128)(2,1)}, bf16[3,1024,64]{2,1,0:T(8,128)(2,...) custom-call(bf16[256,768]{1,0:T(8,128)(2,1)} %bitcast.27, ...), custom_call_target="tpu_custom_call" | custom-call | tf_op jit(solution)/shard_map/forward_part/pallas_call | solution.py:336
  71.6 147.0 %backward_part.1 = (bf16[256,768]{1,0:T(8,128)(2,1)}, bf16[256,768]{1,0:T(8,128)(2,1)}, bf16[192,1024]{1,0:T(8,128)(2,1)}, f32[96,1152]{1,0:T(8,128)}, f32[96,57...) custom-call(f32[8,1024]{1,0:T(8,128)} %pad.17.refs_2_.refs_0_, ...), custom_call_target="tpu_custom_call" | custom-call | tf_op jit(solution)/shard_map/backward_part/pallas_call | solution.py:1033
  218.6 0.0 copy-start.2
  218.7 0.0 copy-start.6
  218.7 1.9 copy.38
  220.6 1.8 copy.49
  222.4 1.8 copy.50
  224.2 1.8 copy.51
  225.9 1.8 copy.52
  227.8 0.7 copy.53
  228.4 0.6 copy.54
  229.1 0.6 copy.55
  229.7 0.0 copy-done.3
  229.7 0.7 copy.56
  230.4 0.0 copy-done.4
  230.4 0.6 copy.57
  231.1 0.0 copy-done.1
  231.1 0.7 copy.58
  (14 shorter events, 0.1 us)
Async XLA Ops:
  5.1 4.9 %copy-start = (bf16[768,2304]{1,0:T(8,128)(2,1)S(1)}, bf16[768,2304]{1,0:T(8,128)(2,1)}, u32[]{:S(2)}) copy-start(bf16[768,2304]{1,0:T(8,128)(2,1)} %refs_28_.1) | copy-start | bytes 10616836
  218.6 9.1 %copy-start.2 = (f32[96,576]{1,0:T(8,128)S(1)}, f32[96,576]{1,0:T(8,128)}, u32[]{:S(2)}) copy-start(f32[96,576]{1,0:T(8,128)} %get-tuple-element.130) | copy-start | bytes 663556
  218.7 9.8 %copy-start.6 = (f32[96,192]{1,0:T(8,128)S(1)}, f32[96,192]{1,0:T(8,128)}, u32[]{:S(2)}) copy-start(f32[96,192]{1,0:T(8,128)} %get-tuple-element.131) | copy-start | bytes 221188
  218.7 10.4 %copy-start.5 = (f32[96,192]{1,0:T(8,128)S(1)}, f32[96,192]{1,0:T(8,128)}, u32[]{:S(2)}) copy-start(f32[96,192]{1,0:T(8,128)} %get-tuple-element.132) | copy-start | bytes 221188
  218.7 11.1 %copy-start.3 = (f32[128,384]{1,0:T(8,128)S(1)}, f32[128,384]{1,0:T(8,128)}, u32[]{:S(2)}) copy-start(f32[128,384]{1,0:T(8,128)} %get-tuple-element.133) | copy-start | bytes 589828
  218.7 11.7 %copy-start.4 = (f32[96,192]{1,0:T(8,128)S(1)}, f32[96,192]{1,0:T(8,128)}, u32[]{:S(2)}) copy-start(f32[96,192]{1,0:T(8,128)} %get-tuple-element.134) | copy-start | bytes 221188
  218.7 12.4 %copy-start.1 = (f32[96,768]{1,0:T(8,128)S(1)}, f32[96,768]{1,0:T(8,128)}, u32[]{:S(2)}) copy-start(f32[96,768]{1,0:T(8,128)} %get-tuple-element.135) | copy-start | bytes 884740

commit v2 on v1

--- a/solution.py
+++ b/solution.py
@@ -124,24 +124,32 @@
     pl.semaphore_wait(barrier, seq - 1 + len(dp_peers))
 
 
-K1_OUTS = tuple(dict(h1=0, qT=0, kT=0, kn=0, vn=0, lse=0, oT=0, aout=0, x1=0, h2T=0, cqT=0, kv=0, ckT=0, lsec=0, coT=0, x2=0, text=0))
-
-
-def forward_kernel(dims, *refs):
+K1_OUTS = tuple(dict(h1=0, qT=0, kT=0, kn=0, vn=0, lse=0, oT=0, aout=0, x1=0, h2T=0, cqT=0, kv=0, ckT=0, lsec=0, coT=0, x2=0, text=0, mods=0, codes=0))
+
+
+def forward_kernel(dims, segs, *refs):
     seq, tok, full, width, keys, group, dc = dims
     hl = H // seq
-    ins, refs = refs[:9], refs[9:]
-    x_hbm, text_hbm, codes, mods, wg_hbm, wckv_hbm, wp_hbm, wcq_hbm, wco_hbm = ins
+    ins, refs = refs[:12], refs[12:]
+    x_hbm, text_hbm, seg_in, pad_in, len_in, emb, wada_hbm, wqkv_hbm, wckv_hbm, wp_hbm, wcq_hbm, wco_hbm = ins
     outs, refs = Bag(zip(K1_OUTS, refs[: len(K1_OUTS)])), refs[len(K1_OUTS) :]
     (
         x_all, text_all, wg, wckv, wp, wcq, wco, qT, kT, vT, kn, vn, lse, osend, orecv, aout, x1, h2T, cqT, kv, kvT,
-        lsec, coT, x2, bias, biasc, kcol, tcol, xin, lsem, ssem, rsem,
+        lsec, coT, x2, bias, biasc, kcol, tcol, xin, wada, mods, codes, lsem, ssem, rsem,
     ) = refs
     local, remote = Local(lsem), Remote(ssem, rsem)
     s = lax.axis_index(SEQ)
     load_x = local.start(x_hbm, xin)
     load_own = local.start(x_hbm, x_all.at[s])
-    load_wg = local.start(wg_hbm, wg)
+    load_ada = local.start(wada_hbm, wada)
+    first = lax.div(s * group, 128) * 128
+    odd = lax.rem(s * group, 128) > 0
+    load_wg = [
+        local.start(
+            wqkv_hbm.at[:, pl.ds(pl.multiple_of(t * width + first, 128), 256)], wg.at[:, pl.ds(t * 256, 256)]
+        )
+        for t in range(3)
+    ]
     load_text = local.start(text_hbm, text_all.at[s])
     load_w = [local.start(a, b) for a, b in ((wckv_hbm, wckv), (wp_hbm, wp), (wcq_hbm, wcq), (wco_hbm, wco))]
     greet(seq, s, ())
@@ -161,11 +169,28 @@
     for k in range(1, seq):
         send_t(k).start()
 
+    tl = keys // seq // segs
+    place = lax.broadcasted_iota(jnp.int32, (1, full), 1).astype(F32)
+    block = jnp.floor((place + 0.5) / tl)
+    owner = jnp.floor((block + 0.5) / segs)
+    clip = block - owner * segs
+    length = jnp.zeros((1, full), F32)
+    for c in range(segs):
+        length = jnp.where(clip == c, jnp.broadcast_to(len_in[0:1, c : c + 1].astype(F32), (1, full)), length)
+    codes[...] = jnp.zeros_like(codes)
+    codes[0:1, :] = seg_in[...].astype(F32)
+    codes[1:2, :] = jnp.where(pad_in[...] == 1, seg_in[...].astype(F32), -1.0)
+    codes[2:3, :] = jnp.where(owner * tl + place - block * tl < length, clip, -1.0)
+    save_codes = local.start(codes, outs.codes)
     kcol[...] = column(codes[1:2, :full])
     tcol[...] = column(codes[2:3, :keys])
     load_x.wait()
     load_own.wait()
-    load_wg.wait()
+    load_ada.wait()
+    mods[...] = nn(emb[...], wada[...])
+    save_mods = local.start(mods, outs.mods)
+    for c in load_wg:
+        c.wait()
 
     def project(k, carry):
         @pl.when(k > 0)
@@ -179,7 +204,14 @@
         n, _ = norm_parts(x_all[at].astype(F32))
         h1 = (n * (1.0 + pick(mods, seg, 1, width)) + pick(mods, seg, 0, width)).astype(BF)
         x_all[at] = h1
-        out = nn(h1, wg[...])
+        wide = nn(h1, wg[...])
+        out = jnp.concatenate(
+            [
+                jnp.where(odd, wide[:, t * 256 + 64 : t * 256 + 64 + group], wide[:, t * 256 : t * 256 + group])
+                for t in range(3)
+            ],
+            axis=1,
+        )
         for h in range(hl):
             kn[h, rows, :] = out[:, group + h * HD : group + (h + 1) * HD].astype(BF)
             vn[h, rows, :] = out[:, 2 * group + h * HD : 2 * group + (h + 1) * HD].astype(BF)
@@ -191,7 +223,7 @@
         return carry
 
     lax.fori_loop(0, seq, project, 0)
-    saves = [
+    saves = [save_mods, save_codes] + [
         local.start(a, b)
         for a, b in ((x_all, outs.h1), (qT, outs.qT), (kT, outs.kT), (kn, outs.kn), (vn, outs.vn))
     ]
@@ -321,22 +353,25 @@
         coT=((width, tok), BF),
         x2=((tok, width), F32),
         text=((seq, keys // seq, dc), BF),
+        mods=((8, 6 * width), F32),
+        codes=((8, full), F32),
     )
     v = pltpu.VMEM
     scratch = [
-        v((seq, tok, width), BF), v((seq, keys // seq, dc), BF), v((width, 3 * group), BF), v((dc, 2 * width), BF),
+        v((seq, tok, width), BF), v((seq, keys // seq, dc), BF), v((width, 3 * 256), BF), v((dc, 2 * width), BF),
         v((width, width), BF), v((width, width), BF), v((width, width), BF),
         v((group, full), BF), v((group, full), BF), v((group, full), BF), v((hl, full, HD), BF), v((hl, full, HD), BF),
         v((8, full), F32), v((seq, group, tok), BF), v((seq, group, tok), BF),
         v((tok, width), F32), v((tok, width), F32), v((width, tok), BF), v((width, tok), BF),
         v((keys, 2 * width), BF), v((2 * width, keys), BF), v((16, tok), F32), v((width, tok), BF), v((tok, width), F32),
         v((full, tok), F32), v((keys, tok), F32), v((full, 128), F32), v((keys, 128), F32), v((tok, width), BF),
+        v((width, 6 * width), BF), v((8, 6 * width), F32), v((8, full), F32),
         pltpu.SemaphoreType.DMA((32,)), pltpu.SemaphoreType.DMA((3 * seq,)), pltpu.SemaphoreType.DMA((3 * seq,)),
     ]
     outs = pl.pallas_call(
-        functools.partial(forward_kernel, dims),
+        functools.partial(forward_kernel, dims, args[4].shape[1]),
         out_shape=[jax.ShapeDtypeStruct(*shapes[n]) for n in K1_OUTS],
-        in_specs=[ANY, ANY, INV, INV, ANY, ANY, ANY, ANY, ANY],
+        in_specs=[ANY, ANY, INV, INV, INV, INV, ANY, ANY, ANY, ANY, ANY, ANY],
         out_specs=[ANY] * len(K1_OUTS),
         scratch_shapes=scratch,
         compiler_params=pltpu.CompilerParams(
@@ -486,6 +521,16 @@
         loads[n] = local.start(r["in_" + n], r[n])
     loads.x = local.start(r.in_x, r.x)
 
+    stores = []
+
+    def stored(n, slot):
+        return pltpu.make_async_copy(r["out_" + n], r["hbm_" + n], r.lsem.at[slot])
+
+    def store(n):
+        stores.append((n, local.used))
+        stored(n, local.used).start()
+        local.used += 1
+
     barrier = pltpu.get_barrier_semaphore()
     for k in range(1, seq):
         pl.semaphore_signal(barrier, inc=1, device_id={SEQ: lax.rem(s + k, seq)}, device_id_type=MESH)
@@ -514,14 +559,21 @@
     def into_cols(n):
         def finish(total):
             r["out_" + n][...] = total
+            store(n)
 
         return finish
 
     def into_pack(n):
         def finish(total):
             rows, lanes = total.shape
-            r["out_" + n][0:rows, :] = total[:, : lanes // 2]
-            r["out_" + n][rows : 2 * rows, :] = total[:, lanes // 2 :]
+            if n == "fc2":
+                turned = total.T
+                r.out_fc2[:, 0:rows] = turned[: lanes // 2]
+                r.out_fc2[:, rows : 2 * rows] = turned[lanes // 2 :]
+            else:
+                r["out_" + n][0:rows, :] = total[:, : lanes // 2]
+                r["out_" + n][rows : 2 * rows, :] = total[:, lanes // 2 :]
+            store(n)
 
         return finish
 
@@ -629,6 +681,7 @@
             m = m_ref[...]
             x2w = r.x2[...]
             r.out_block_out[...] = (x2w + pick(mods, seg, 5, width) * m).astype(BF)
+            store("block_out")
             clip_sum(5, dy * m)
             dh = dh_ref[...]
             nw, rstd = norm_parts(x2w)
@@ -827,6 +880,7 @@
             dm_copies.append(remote.start(describe_dm))
         back = norm_back(dh1 * (1.0 + pick(mods, seg, 1, width)), nx, rstd)
         r.out_grad_frames[...] = (r.dx[...] + back).astype(BF)
+        store("grad_frames")
         grads.ckv.step()
         grads.qkv.step()
         grads.cq.step()
@@ -854,6 +908,7 @@
         for b in range(1, seq):
             gt = gt + nt(r.dkvl[b], wckv[:, b * quarter : (b + 1) * quarter])
         r.out_grad_text[...] = gt.astype(BF)
+        store("grad_text")
         grads.fc2.step()
         grads.cout.step()
         grads.qkv.step()
@@ -905,6 +960,7 @@
         rest = (allm - high.astype(F32)).astype(BF)
         ga = tn(emb, high) + tn(emb, rest)
         r.out_ada[...] = ga[: width // dp]
+        store("ada")
         for j in range(3):
             src = lax.rem(3 * s + j, seq)
 
@@ -913,6 +969,7 @@
                 remote.make(r.fq.at[j], r.rq.at[j], q_base + j, {SEQ: src}).wait_recv()
 
             r.out_qkv[:, j * group : (j + 1) * group] = r.rq[j]
+        store("qkv")
 
         for t in range(3):
             to, slot, copy = send_q(t)
@@ -934,6 +991,8 @@
         lax.fori_loop(1, dp, wait_sent, 0)
         for c in remote.open:
             c().wait_send()
+        for n, slot in stores:
+            stored(n, slot).wait()
 
     pl.run_scoped(
         tail,
@@ -968,8 +1027,8 @@
             ins.append(value)
             specs.append(spec)
 
-    add_in(codes=args.codes, spec=INV)
-    add_in(mods=args.mods, spec=INV)
+    add_in(codes=fwd.codes, spec=INV)
+    add_in(mods=fwd.mods, spec=INV)
     add_in(in_x=args.x)
     add_in(in_cot=args.cot)
     add_in(in_emb=args.emb)
@@ -991,10 +1050,10 @@
         ckv=((dc // BLOCKS, 2 * width // seq), F32),
         cout=((block, group), F32),
         fc1=((block, ff // seq), F32),
-        fc2=((ff // BLOCKS, group), F32),
+        fc2=((group, ff // BLOCKS), F32),
     )
     for n in K2_OUTS:
-        names.append("out_" + n)
+        names.append("hbm_" + n)
     scratch = []
 
     def add(**kw):
@@ -1002,6 +1061,8 @@
             names.append(name)
             scratch.append(v(shape, dtype))
 
+    for n in K2_OUTS:
+        add(**{"out_" + n: outs[n]})
     add(cot=((tok, width), BF))
     add(x=((tok, width), BF))
     for n in K2_LOADS:
@@ -1027,20 +1088,47 @@
     add(fq=((3, block, group), F32))
     add(rq=((3, block, group), F32))
     count = 2 * dp + 64
-    for n, k in dict(lsem=40, ssem=count, rsem=count).items():
+    for n, k in dict(lsem=64, ssem=count, rsem=count).items():
         names.append(n)
         scratch.append(pltpu.SemaphoreType.DMA((k,)))
     got = pl.pallas_call(
         functools.partial(backward_kernel, dims, tuple(names), dp),
         out_shape=[jax.ShapeDtypeStruct(*outs[n]) for n in K2_OUTS],
         in_specs=specs,
-        out_specs=[INV] * len(K2_OUTS),
+        out_specs=[ANY] * len(K2_OUTS),
         scratch_shapes=scratch,
         compiler_params=pltpu.CompilerParams(
             collective_id=1, has_side_effects=True, vmem_limit_bytes=67043328
         ),
         name="backward_part",
     )(*ins)
+    return Bag(zip(K2_OUTS, got))
+
+
+def hand_over(*refs):
+    count = len(K2_OUTS)
+    ins, outs, held, sems = refs[:count], refs[count : 2 * count], refs[2 * count : -1], refs[-1]
+    first = [pltpu.make_async_copy(a, b, sems.at[0, i]) for i, (a, b) in enumerate(zip(ins, held))]
+    second = [pltpu.make_async_copy(a, b, sems.at[1, i]) for i, (a, b) in enumerate(zip(held, outs))]
+    for c in first:
+        c.start()
+    for c, n in zip(first, second):
+        c.wait()
+        n.start()
+    for c in second:
+        c.wait()
+
+
+def run_hand_over(g):
+    values = [g[n] for n in K2_OUTS]
+    got = pl.pallas_call(
+        hand_over,
+        out_shape=[jax.ShapeDtypeStruct(a.shape, a.dtype) for a in values],
+        in_specs=[ANY] * len(values),
+        out_specs=[ANY] * len(values),
+        scratch_shapes=[pltpu.VMEM(a.shape, a.dtype) for a in values] + [pltpu.SemaphoreType.DMA((2, len(values)))],
+        name="hand_over",
+    )(*values)
     return Bag(zip(K2_OUTS, got))
 
 
@@ -1056,45 +1144,27 @@
     keys = segs * tl * seq
     group = (H // seq) * HD
     dims = (seq, tok, full, width, keys, group, dc)
-    s = lax.axis_index(SEQ)
-
-    emb = embed_steps(step_ids[0], width).astype(BF)
-    mods = jnp.dot(emb, w_ada, preferred_element_type=F32)
-    mods = jnp.pad(mods, ((0, 8 - segs), (0, 0)))
+    emb = embed_steps(jnp.pad(step_ids[0], (0, 8 - segs)), width).astype(BF)
     span = width // dp
-    emb_parts = jnp.pad(
-        jnp.swapaxes(emb.reshape(segs, dp, span), 0, 1), ((0, 0), (0, 8 - segs), (0, 128 - span))
-    )
-    place = jnp.arange(keys)
-    clip = (place // tl) % segs
-    position = (place // (tl * segs)) * tl + place % tl
-    length = jnp.sum(jnp.where(clip[None, :] == jnp.arange(segs)[:, None], text_len[0][:, None], 0), axis=0)
-    text_code = jnp.where(position < length, clip, -1)
-    codes = jnp.stack(
-        [seg_ids[0], jnp.where(padding[0] == 1, seg_ids[0], -1), jnp.pad(text_code, (0, full - keys))]
-    ).astype(F32)
-    codes = jnp.pad(codes, ((0, 5), (0, 0)))
+    emb_parts = jnp.pad(jnp.swapaxes(emb.reshape(8, dp, span), 0, 1), ((0, 0), (0, 0), (0, 128 - span)))
     x = frames[0]
     text = text_states.reshape(segs * tl, dc)
-    w_group = lax.dynamic_index_in_dim(
-        w_qkv.reshape(width, 3, seq, group), s, 2, keepdims=False
-    ).reshape(width, 3 * group)
-    fwd = run_forward(dims, (x, text, codes, mods, w_group, w_ckv, w_proj, w_cq, w_cout))
+    fwd = run_forward(dims, (x, text, seg_ids, padding, text_len, emb, w_ada, w_qkv, w_ckv, w_proj, w_cq, w_cout))
     args = Bag(
-        codes=codes, mods=mods, x=x, cot=cotangent[0], emb=emb_parts, ckv=w_ckv, qkv=w_qkv,
+        x=x, cot=cotangent[0], emb=emb_parts, ckv=w_ckv, qkv=w_qkv,
         fc1=w_fc1, fc2=w_fc2, cout=w_cout, cq=w_cq, proj=w_proj,
     )
-    g = run_backward(dims, dp, fwd, args)
+    g = run_hand_over(run_backward(dims, dp, fwd, args))
     stride = dp // BLOCKS
     if stride > 1:
         groups = [[b * stride + j for j in range(stride)] for b in range(BLOCKS)]
         for n in GRADS:
-            g[n] = lax.psum_scatter(g[n], DP, scatter_dimension=0, axis_index_groups=groups, tiled=True)
+            g[n] = lax.psum_scatter(g[n], DP, scatter_dimension=1 if n == "fc2" else 0, axis_index_groups=groups, tiled=True)
     return (
         g.block_out.reshape(frames.shape),
         g.grad_frames.reshape(frames.shape),
         g.grad_text.reshape(text_states.shape),
-        g.ada, g.qkv, g.proj, g.cq, g.ckv, g.cout, g.fc1, g.fc2,
+        g.ada, g.qkv, g.proj, g.cq, g.ckv, g.cout, g.fc1, g.fc2.T,
     )
 
 

time: 232 us -> 208 us (0.90)
  local copies, waits for them, and re-layouts: 21.1 us -> 0.61 us
  matrix products: 4.17 us -> 0 us
    unnamed x26 -> x0, local copies, waits for them, and re-layouts: 16.6 us -> none
    dot_general x1 -> x0, matrix products: 4.17 us -> none  [per_device(): mods = jnp.dot(emb, w_ada, preferred_element_type=F32)]
    pallas_call x1 -> x2, Pallas kernels: 55.6 us -> 58.2 us  [the longest x1 55.4 us: run_forward(): pl.pallas_call(functools.partial(forward_kernel, dims, args[4].shape[1]),...]
where the time goes in v2:
time: 208 us; the launch traced here: 207 us
  Pallas kernels  204 us (98%)
    pallas_call x1, Pallas kernels, run_backward(): pl.pallas_call(functools.partial(backward_kernel, dims, tuple(names), dp)...  146 us
    pallas_call x1, Pallas kernels, run_forward(): pl.pallas_call(functools.partial(forward_kernel, dims, args[4].shape[1]),...  55.4 us

profile of v2, /device:TPU:0, one launch (start us, length us, event | category | flops | bytes accessed | tf_op | source)
XLA Modules:
  0.0 207.5 jit_solution(14011017681478142816)
XLA Ops:
  0.6 0.7 pad_convert_fusion
  1.3 0.1 multiply_cosine_fusion.1
  1.5 0.6 multiply_convert_fusion.1.refs_5_
  2.1 0.1 multiply_cosine_fusion
  2.3 0.6 pad.9.refs_4_
  2.9 55.4 %forward_part.1 = (bf16[4,256,768]{2,1,0:T(8,128)(2,1)}, bf16[192,1024]{1,0:T(8,128)(2,1)}, bf16[192,1024]{1,0:T(8,128)(2,1)}, bf16[3,1024,64]{2,1,0:T(8,128)(2,...) custom-call(bf16[256,768]{1,0:T(8,128)(2,1)} %bitcast.20, ...), custom_call_target="tpu_custom_call" | custom-call | tf_op jit(solution)/shard_map/forward_part/pallas_call | solution.py:371
  58.3 146.2 %backward_part.1 = (bf16[256,768]{1,0:T(8,128)(2,1)}, bf16[256,768]{1,0:T(8,128)(2,1)}, bf16[192,1024]{1,0:T(8,128)(2,1)}, f32[96,1152]{1,0:T(8,128)}, f32[96,57...) custom-call(f32[8,1024]{1,0:T(8,128)} %get-tuple-element.52.refs_0_,, ...), custom_call_target="tpu_custom_call" | custom-call | tf_op jit(solution)/shard_map/backward_part/pallas_call | solution.py:1094
  204.5 2.8 %hand_over.1 = (bf16[256,768]{1,0:T(8,128)(2,1)}, bf16[256,768]{1,0:T(8,128)(2,1)}, bf16[192,1024]{1,0:T(8,128)(2,1)}, f32[96,1152]{1,0:T(8,128)}, f32[96,576]{1...) custom-call(bf16[256,768]{1,0:T(8,128)(2,1)} %get-tuple-element.71.r, ...), custom_call_target="tpu_custom_call" | custom-call | tf_op jit(solution)/shard_map/hand_over/pallas_call | solution.py:1124
  (3 shorter events, 0.0 us)

commit v3 on v2

--- a/solution.py
+++ b/solution.py
@@ -13,7 +13,8 @@
 BLOCKS = 8
 SEQ = "seq"
 DP = "dp"
-CUT, COLS, PACK = 3, 1, 2
+COLS, PACK = 1, 2
+CUT, XY1, XY2, L0, L1, L2 = 3, 4, 5, 6, 7, 8
 BF = jnp.bfloat16
 F32 = jnp.float32
 MESH = pl.DeviceIdType.MESH
@@ -90,15 +91,25 @@
             device_id_type=MESH,
         )
 
-    def start(self, describe):
+    def start(self, describe, when=None):
         slot = self.slots(1)
 
         def again():
             src, dst, where = describe()
             return self.make(src, dst, slot, where)
 
-        again().start()
-        self.open.append(again)
+        def launch():
+            again().start()
+
+        def sent():
+            again().wait_send()
+
+        if when is None:
+            launch()
+            self.open.append(sent)
+        else:
+            pl.when(when())(launch)
+            self.open.append(lambda: pl.when(when())(sent))
         return again
 
 
@@ -385,7 +396,7 @@
 class Grad:
     def __init__(self, ref, kind, order, bufs, where, remote, finish):
         self.ref, self.kind, self.order, self.bufs = ref, kind, order, bufs
-        self.s, self.seq, self.d, self.stride, self.bits = where
+        self.s, self.seq, self.d, self.stride, self.bits, self.flip, self.dp = where
         self.remote, self.finish = remote, finish
         self.fixed, self.cut, self.stage, self.copies = {}, False, 0, []
 
@@ -408,10 +419,76 @@
                 index += [lax.div(quarter, 2), slice(None), lanes]
         return self.ref.at[tuple(index)]
 
+    def line(self):
+        return 2 * self.bits[2] + self.bits[1]
+
+    def chunk(self, fixed, quarter, number):
+        number = lax.rem(number, 4)
+        return self.view({**fixed, 2: lax.div(number, 2), 1: lax.rem(number, 2)}, quarter)
+
+    def end_halving(self, what, buf):
+        for a in range(2):
+            for w in range(2 if what == XY1 else 1):
+                owner = self.flip[2 - a] if w else self.s
+
+                def add(b, carry):
+                    own = self.view({**self.fixed, 2: a}, owner, [b])
+                    more = buf[a, w, b] if what == XY1 else buf[a, b]
+                    own[...] = (own[...].astype(F32) + more.astype(F32)).astype(BF)
+                    return carry
+
+                lax.fori_loop(0, 2, add, 0)
+
+    def end_line(self, t, buf):
+        quarter, line = self.s if self.cut else None, self.line()
+        above, below = self.copies
+
+        def take(copy, side, number):
+            copy().wait_recv()
+            own = self.chunk(self.fixed, quarter, number)
+            own[...] = (own[...].astype(F32) + buf[side].astype(F32)).astype(BF)
+
+        @pl.when((line >= 1) & (line <= t + 1))
+        def _():
+            take(above, 0, line + 2 - t)
+
+        @pl.when((line <= 2) & (line >= 2 - t))
+        def _():
+            take(below, 1, line + 2 + t)
+
     def begin(self):
         what, buf = self.order[self.stage], self.bufs[self.stage]
         self.copies = []
-        if what == CUT:
+        if what == XY1:
+            for a in range(2):
+                to = self.flip[1 + a]
+                for w, owner in enumerate((to, self.flip[3])):
+
+                    def describe(a=a, w=w, owner=owner, to=to, fixed=dict(self.fixed)):
+                        return self.view({**fixed, 2: a}, owner), buf.at[a, w], {SEQ: to}
+
+                    self.copies.append(self.remote.start(describe))
+        elif what == XY2:
+            for a in range(2):
+
+                def describe(a=a, to=self.flip[2 - a], fixed=dict(self.fixed)):
+                    return self.view({**fixed, 2: a}, to), buf.at[a], {SEQ: to}
+
+                self.copies.append(self.remote.start(describe))
+        elif what >= L0:
+            t = what - L0
+
+            def upward(fixed=dict(self.fixed), quarter=self.s if self.cut else None):
+                peer = lax.rem(self.d + 2 * self.stride, self.dp)
+                return self.chunk(fixed, quarter, self.line() + 3 - t), buf.at[0], {DP: peer}
+
+            def downward(fixed=dict(self.fixed), quarter=self.s if self.cut else None):
+                peer = lax.rem(self.d - 2 * self.stride + self.dp, self.dp)
+                return self.chunk(fixed, quarter, self.line() + 1 + t), buf.at[1], {DP: peer}
+
+            self.copies.append(self.remote.start(upward, lambda: self.line() <= t))
+            self.copies.append(self.remote.start(downward, lambda: self.line() >= 3 - t))
+        elif what == CUT:
             for k in range(1, self.seq):
 
                 def describe(k=k, fixed=dict(self.fixed)):
@@ -430,8 +507,19 @@
 
     def end(self):
         what, buf = self.order[self.stage], self.bufs[self.stage]
+        if what >= L0:
+            self.end_line(what - L0, buf)
+            self.stage += 1
+            if what == L2:
+                self.fixed[1], self.fixed[2] = self.bits[1], self.bits[2]
+            return
         for c in self.copies:
             c().wait_recv()
+        if what in (XY1, XY2):
+            self.end_halving(what, buf)
+            self.stage += 1
+            self.cut = what == XY2
+            return
         if what == CUT:
             self.cut = True
         else:
@@ -472,27 +560,31 @@
 def grad_buffers(shape, kind, order, seq):
     lead, payload, out, cut, free = 3, list(shape), [], False, 3
     for what in order:
-        if what == CUT:
+        if what in (CUT, XY1, XY2):
             cut = True
-        else:
+        elif what in (0, 1, 2):
             free -= 1
+        elif what == L2:
+            free = 0
         p = list(payload)
         if cut:
             if kind == COLS:
                 p[-1] //= seq
             else:
                 p = [p[1], p[2] // 2]
-        head = [seq - 1] if what == CUT else []
-        out.append(pltpu.VMEM(tuple(head + [2] * free + p), BF))
+        head = {CUT: [seq - 1], XY1: [2, 2, 2], XY2: [2, 2], L0: [2], L1: [2], L2: [2]}.get(what, [])
+        if what in (CUT, 0, 1, 2):
+            head = head + [2] * free
+        out.append(pltpu.VMEM(tuple(head + p), BF))
     return out
 
 
 GRADS = dict(
-    fc2=(PACK, (0, CUT, 1, 2)),
-    fc1=(COLS, (0, 1, 2, CUT)),
-    cout=(PACK, (0, CUT, 1, 2)),
-    cq=(PACK, (0, CUT, 1, 2)),
-    proj=(PACK, (0, CUT, 1, 2)),
+    fc2=(PACK, (0, XY1, XY2, 1, 2)),
+    fc1=(COLS, (0, L0, L1, L2, CUT)),
+    cout=(PACK, (0, XY1, XY2, 1, 2)),
+    cq=(PACK, (0, XY1, XY2, 1, 2)),
+    proj=(PACK, (0, XY1, XY2, 1, 2)),
     ckv=(None, (0, 1, 2)),
     qkv=(None, (0, 1, 2)),
 )
@@ -509,7 +601,9 @@
     local, remote = Local(r.lsem), Remote(r.ssem, r.rsem)
     s, d = lax.axis_index(SEQ), lax.axis_index(DP)
     bits = [lax.rem(lax.div(d, stride << b), 2) for b in range(3)]
-    where = (s, seq, d, stride, bits)
+    sx, sy = lax.rem(s, 2), lax.div(s, 2)
+    flip = [s, s + 1 - 2 * sx, s + 2 - 4 * sy, 3 - s]
+    where = (s, seq, d, stride, bits, flip, dp)
     codes, mods = r.codes, r.mods
 
     loads = Bag()
@@ -628,6 +722,40 @@
     def send_do(k):
         to = lax.rem(s + k, seq)
         return remote.make(r.dosend.at[to], r.dorecv.at[s], do_base + k, {SEQ: to})
+
+    def kv_part(a, owner):
+        lanes = pl.ds(pl.multiple_of(owner * quarter, quarter), quarter)
+        return r.kv.at[pl.ds(a * keys // 2, keys // 2), lanes]
+
+    def begin_kv():
+        for a in range(2):
+            for w, owner in enumerate((flip[1 + a], flip[3])):
+
+                def describe(a=a, w=w, owner=owner):
+                    return kv_part(a, owner), r.dkvr.at[a, w], {SEQ: flip[1 + a]}
+
+                dkv_copies.append(remote.start(describe))
+
+    def step_kv():
+        for c in dkv_copies:
+            c().wait_recv()
+        dkv_copies.clear()
+        for a in range(2):
+            for w, owner in enumerate((s, flip[2 - a])):
+                own = kv_part(a, owner)
+                own[...] = (own[...].astype(F32) + r.dkvr[a, w].astype(F32)).astype(BF)
+
+            def describe(a=a):
+                return kv_part(a, flip[2 - a]), r.dkvs.at[a], {SEQ: flip[2 - a]}
+
+            dkv_copies.append(remote.start(describe))
+
+    def end_kv():
+        for c in dkv_copies:
+            c().wait_recv()
+        for a in range(2):
+            own = kv_part(a, s)[...].astype(F32) + r.dkvs[a].astype(F32)
+            r.dkvq[a * seq // 2 : (a + 1) * seq // 2] = own.astype(BF).reshape(seq // 2, tl, quarter)
 
     def middle(*held):
         for n, ref in zip(K2_HELD, held):
@@ -702,7 +830,6 @@
             tcol = column(codes[2:3, :keys])
             biasc[...] = jnp.where(jnp.broadcast_to(tcol[:, :1], (keys, tok)) == seg_row, 0.0, MASKED)
             grads.fc2.step()
-            grads.fc1.step()
             kv = r.kv
 
             def pair(p, carry):
@@ -725,7 +852,10 @@
                 kv[:, vcols] = jnp.concatenate(parts_v, axis=1).astype(BF)
                 return carry
 
-            lax.fori_loop(0, H // 2, pair, 0)
+            lax.fori_loop(0, 2, pair, 0)
+            grads.fc1.step()
+            lax.fori_loop(2, H // 2, pair, 0)
+            begin_kv()
             dcq = dcqT[...].T.astype(BF)
             loads.w_cq.wait()
             loads.h2T.wait()
@@ -751,17 +881,8 @@
         clip_sum(2, dx1 * r.aout[...])
         square("proj", lambda i: r.oT[i], da)
         grads.proj.begin()
-        grads.cout.step()
+        grads.fc2.step()
         grads.fc1.step()
-        for k in range(1, seq):
-
-            def describe_kv(k=k):
-                to = lax.rem(s + k, seq)
-                lanes = pl.ds(pl.multiple_of(to * quarter, quarter), quarter)
-                return r.kv.at[:, lanes], r.dkvr.at[k - 1], {SEQ: to}
-
-            dkv_copies.append(remote.start(describe_kv))
-        grads.fc2.step()
         for c in (loads.qT, loads.kT, loads.kn, loads.vn, loads.lse):
             c.wait()
 
@@ -794,7 +915,9 @@
                     r.dqs[at, :, hs] = dq.T.astype(BF)
                 return carry
 
-            lax.fori_loop(0, seq, block, 0)
+            lax.fori_loop(0, 2, block, 0)
+            step_kv()
+            lax.fori_loop(2, seq, block, 0)
             for h in range(hl):
                 for b in range(seq):
                     br = slice(b * tok, (b + 1) * tok)
@@ -820,6 +943,10 @@
 
     for k in range(1, seq):
         send_dq(k).start()
+    for n in ("cout", "cq", "proj"):
+        grads[n].step()
+    grads.fc2.step()
+    grads.fc1.step()
     r.dqr[s] = r.dqs[s]
 
     def tail(h1, text, wqkv, wckv, dqf):
@@ -832,17 +959,7 @@
         gq = tn(h1[...].reshape(full, width), r.dqs[...].reshape(full, 3 * group))
         r.g_qkv[...] = gq.astype(BF).reshape(2, 2, 2, width // BLOCKS, 3 * group)
         grads.qkv.begin()
-        grads.cq.step()
-        grads.proj.step()
-        grads.fc2.step()
-        grads.cout.step()
-        grads.fc1.step()
-        for c in dkv_copies:
-            c().wait_recv()
-        own = r.kv[:, pl.ds(pl.multiple_of(s * quarter, quarter), quarter)].astype(F32)
-        for k in range(seq - 1):
-            own = own + r.dkvr[k].astype(F32)
-        r.dkvq[...] = own.astype(BF).reshape(seq, tl, quarter)
+        end_kv()
         kv_base = remote.slots(seq)
 
         def send_kv(k):
@@ -881,10 +998,12 @@
         back = norm_back(dh1 * (1.0 + pick(mods, seg, 1, width)), nx, rstd)
         r.out_grad_frames[...] = (r.dx[...] + back).astype(BF)
         store("grad_frames")
+        grads.fc1.step()
         grads.ckv.step()
         grads.qkv.step()
-        grads.cq.step()
-        grads.proj.step()
+        for n in ("cout", "cq", "proj"):
+            grads[n].step()
+        grads.fc2.step()
         for c in dm_copies:
             c().wait_recv()
         total = r.dmod[:, pl.ds(pl.multiple_of(s * part, part), part)]
@@ -909,8 +1028,6 @@
             gt = gt + nt(r.dkvl[b], wckv[:, b * quarter : (b + 1) * quarter])
         r.out_grad_text[...] = gt.astype(BF)
         store("grad_text")
-        grads.fc2.step()
-        grads.cout.step()
         grads.qkv.step()
         q_base = remote.slots(3)
 
@@ -938,14 +1055,8 @@
             def _():
                 r.rq[slot] = r.fq[t]
 
-        grads.ckv.step()
-        grads.cq.step()
-        grads.proj.step()
-        grads.fc1.step()
-        grads.cout.step()
-        grads.ckv.step()
-        grads.cq.step()
-        grads.proj.step()
+        for n in ("cout", "cq", "proj", "ckv", "fc2", "cout", "cq", "proj", "ckv", "fc1", "cout", "cq", "proj"):
+            grads[n].step()
 
         def wait_dm(j, carry):
             send_dm(j).wait_recv()
@@ -989,8 +1100,8 @@
             return carry
 
         lax.fori_loop(1, dp, wait_sent, 0)
-        for c in remote.open:
-            c().wait_send()
+        for sent in remote.open:
+            sent()
         for n, slot in stores:
             stored(n, slot).wait()
 
@@ -1074,7 +1185,8 @@
             scratch.append(b)
     quarter = 2 * width // seq
     add(dx=((tok, width), F32))
-    add(dkvr=((seq - 1, keys, quarter), BF))
+    add(dkvr=((2, 2, keys // 2, quarter), BF))
+    add(dkvs=((2, keys // 2, quarter), BF))
     add(dkvq=((seq, tl, quarter), BF))
     add(dkvl=((seq, tl, quarter), BF))
     add(dosend=((seq, group, tok), BF))
@@ -1087,7 +1199,7 @@
     add(emball=((dp, 8, 128), BF))
     add(fq=((3, block, group), F32))
     add(rq=((3, block, group), F32))
-    count = 2 * dp + 64
+    count = 2 * dp + 96
     for n, k in dict(lsem=64, ssem=count, rsem=count).items():
         names.append(n)
         scratch.append(pltpu.SemaphoreType.DMA((k,)))

time: 208 us -> 185 us (0.89)
  Pallas kernels: 204 us -> 181 us
    pallas_call x1, Pallas kernels: 146 us -> 123 us  [run_backward(): pl.pallas_call(functools.partial(backward_kernel, dims, tuple(names), dp)...]
where the time goes in v3:
time: 185 us
  Pallas kernels  181 us (98%)
    pallas_call x1, Pallas kernels, run_backward(): pl.pallas_call(functools.partial(backward_kernel, dims, tuple(names), dp)...  123 us
    pallas_call x1, Pallas kernels, run_forward(): pl.pallas_call(functools.partial(forward_kernel, dims, args[4].shape[1]),...  55.4 us

profile of v3, /device:TPU:0, one launch (start us, length us, event | category | flops | bytes accessed | tf_op | source)
XLA Modules:
  0.0 184.5 jit_solution(9262771454090866447)
XLA Ops:
  0.6 0.7 pad_convert_fusion
  1.3 0.1 multiply_cosine_fusion.1
  1.5 0.6 multiply_convert_fusion.1.refs_5_
  2.1 0.1 multiply_cosine_fusion
  2.3 0.6 pad.9.refs_4_
  2.9 55.4 %forward_part.1 = (bf16[4,256,768]{2,1,0:T(8,128)(2,1)}, bf16[192,1024]{1,0:T(8,128)(2,1)}, bf16[192,1024]{1,0:T(8,128)(2,1)}, bf16[3,1024,64]{2,1,0:T(8,128)(2,...) custom-call(bf16[256,768]{1,0:T(8,128)(2,1)} %bitcast.20, ...), custom_call_target="tpu_custom_call" | custom-call | tf_op jit(solution)/shard_map/forward_part/pallas_call | solution.py:382
  58.3 123.2 %backward_part.1 = (bf16[256,768]{1,0:T(8,128)(2,1)}, bf16[256,768]{1,0:T(8,128)(2,1)}, bf16[192,1024]{1,0:T(8,128)(2,1)}, f32[96,1152]{1,0:T(8,128)}, f32[96,57...) custom-call(f32[8,1024]{1,0:T(8,128)} %get-tuple-element.52.refs_0_,, ...), custom_call_target="tpu_custom_call" | custom-call | tf_op jit(solution)/shard_map/backward_part/pallas_call | solution.py:1206
  181.6 2.8 %hand_over.1 = (bf16[256,768]{1,0:T(8,128)(2,1)}, bf16[256,768]{1,0:T(8,128)(2,1)}, bf16[192,1024]{1,0:T(8,128)(2,1)}, f32[96,1152]{1,0:T(8,128)}, f32[96,576]{1...) custom-call(bf16[256,768]{1,0:T(8,128)(2,1)} %get-tuple-element.71.r, ...), custom_call_target="tpu_custom_call" | custom-call | tf_op jit(solution)/shard_map/hand_over/pallas_call | solution.py:1236
  (3 shorter events, 0.0 us)

commit v4 on v3

--- a/solution.py
+++ b/solution.py
@@ -146,7 +146,7 @@
     outs, refs = Bag(zip(K1_OUTS, refs[: len(K1_OUTS)])), refs[len(K1_OUTS) :]
     (
         x_all, text_all, wg, wckv, wp, wcq, wco, qT, kT, vT, kn, vn, lse, osend, orecv, aout, x1, h2T, cqT, kv, kvT,
-        lsec, coT, x2, bias, biasc, kcol, tcol, xin, wada, mods, codes, lsem, ssem, rsem,
+        lsec, coT, x2, bias, biasc, kcol, tcol, xin, wada, mods, codes, h1_all, lsem, ssem, rsem,
     ) = refs
     local, remote = Local(lsem), Remote(ssem, rsem)
     s = lax.axis_index(SEQ)
@@ -165,20 +165,25 @@
     load_w = [local.start(a, b) for a, b in ((wckv_hbm, wckv), (wp_hbm, wp), (wcq_hbm, wcq), (wco_hbm, wco))]
     greet(seq, s, ())
 
-    base_x = remote.slots(seq)
-    base_t = remote.slots(seq)
-    base_o = remote.slots(seq)
-
-    def send_x(k):
-        return remote.make(x_hbm, x_all.at[s], base_x + k, {SEQ: lax.rem(s + k, seq)})
-
-    def send_t(k):
-        return remote.make(text_hbm, text_all.at[s], base_t + k, {SEQ: lax.rem(s + k, seq)})
-
-    for k in range(1, seq):
-        send_x(k).start()
-    for k in range(1, seq):
-        send_t(k).start()
+    base_x = remote.slots(5)
+    base_t = remote.slots(5)
+    base_o = remote.slots(4)
+    sx, sy = lax.rem(s, 2), lax.div(s, 2)
+
+    def other(k):
+        kx, ky = (k % 2, k // 2) if isinstance(k, int) else (lax.rem(k, 2), lax.div(k, 2))
+        return 2 * (sy + ky - 2 * sy * ky) + sx + kx - 2 * sx * kx
+
+    def direct(src, held, base, m):
+        return remote.make(src, held.at[s], base + m, {SEQ: other(m)})
+
+    def relay(held, base, m):
+        half = held.shape[1] // 2
+        part = held.at[other(3 - m), pl.ds((m - 1) * half, half)]
+        return remote.make(part, part, base + 2 + m, {SEQ: other(m)})
+
+    for m in (1, 2):
+        direct(x_hbm, x_all, base_x, m).start()
 
     tl = keys // seq // segs
     place = lax.broadcasted_iota(jnp.int32, (1, full), 1).astype(F32)
@@ -204,17 +209,27 @@
         c.wait()
 
     def project(k, carry):
-        @pl.when(k > 0)
+        @pl.when(k == 1)
         def _():
-            send_x(k).wait_recv()
-
-        at = lax.rem(s - k + seq, seq)
+            for m in (1, 2):
+                direct(x_hbm, x_all, base_x, m).wait_recv()
+            for m in (1, 2):
+                relay(x_all, base_x, m).start()
+            for m in (1, 2):
+                direct(text_hbm, text_all, base_t, m).start()
+
+        @pl.when(k == 3)
+        def _():
+            for m in (1, 2):
+                relay(x_all, base_x, m).wait_recv()
+
+        at = other(k)
         rows = pl.ds(pl.multiple_of(at * tok, tok), tok)
         seg = column(codes[0:1, rows])[:, :1]
         seg = jnp.broadcast_to(seg, (tok, width))
         n, _ = norm_parts(x_all[at].astype(F32))
         h1 = (n * (1.0 + pick(mods, seg, 1, width)) + pick(mods, seg, 0, width)).astype(BF)
-        x_all[at] = h1
+        h1_all[at] = h1
         wide = nn(h1, wg[...])
         out = jnp.concatenate(
             [
@@ -236,15 +251,22 @@
     lax.fori_loop(0, seq, project, 0)
     saves = [save_mods, save_codes] + [
         local.start(a, b)
-        for a, b in ((x_all, outs.h1), (qT, outs.qT), (kT, outs.kT), (kn, outs.kn), (vn, outs.vn))
+        for a, b in ((h1_all, outs.h1), (qT, outs.qT), (kT, outs.kT), (kn, outs.kn), (vn, outs.vn))
     ]
 
     def send_o(k):
-        at = lax.rem(s + k, seq)
+        at = other(k)
         return remote.make(osend.at[at], orecv.at[s], base_o + k, {SEQ: at})
 
     def attend(k, carry):
-        at = lax.rem(s + 1 + k, seq)
+        @pl.when(k == 3)
+        def _():
+            for m in (1, 2):
+                direct(text_hbm, text_all, base_t, m).wait_recv()
+            for m in (1, 2):
+                relay(text_all, base_t, m).start()
+
+        at = other(3 - k)
         rows = pl.ds(pl.multiple_of(at * tok, tok), tok)
         seg = codes[0:1, rows]
         row_id = lax.broadcasted_iota(jnp.int32, (full, tok), 0)
@@ -267,7 +289,7 @@
 
         @pl.when(k < seq - 1)
         def _():
-            send_o(k + 1).start()
+            send_o(3 - k).start()
 
         return carry
 
@@ -275,20 +297,24 @@
     orecv[s] = osend[s]
 
     load_text.wait()
-    for k in range(1, seq):
-        send_t(k).wait_recv()
-    saves.append(local.start(text_all, outs.text))
     saves.append(local.start(lse, outs.lse))
     for c in load_w:
         c.wait()
     tl = keys // seq
 
-    def project_text(b, carry):
+    def project_text(k, carry):
+        @pl.when(k == 3)
+        def _():
+            for m in (1, 2):
+                relay(text_all, base_t, m).wait_recv()
+
+        b = other(k)
         trows = pl.ds(pl.multiple_of(b * tl, tl), tl)
         kv[trows, :] = nn(text_all[b], wckv[...]).astype(BF)
         return carry
 
     lax.fori_loop(0, seq, project_text, 0)
+    saves.append(local.start(text_all, outs.text))
 
     def turn_text(c, carry):
         cols = pl.ds(pl.multiple_of(c * 256, 256), 256)
@@ -335,9 +361,12 @@
     lax.fori_loop(0, H // 2, cross, 0)
     x2[...] = x1[...] + tn(coT[...], wco[...])
     saves += [local.start(a, b) for a, b in ((lsec, outs.lsec), (coT, outs.coT), (x2, outs.x2))]
+    for m in (1, 2):
+        direct(x_hbm, x_all, base_x, m).wait_send()
+        relay(x_all, base_x, m).wait_send()
+        direct(text_hbm, text_all, base_t, m).wait_send()
+        relay(text_all, base_t, m).wait_send()
     for k in range(1, seq):
-        send_x(k).wait_send()
-        send_t(k).wait_send()
         send_o(k).wait_send()
     for c in saves:
         c.wait()
@@ -376,8 +405,8 @@
         v((tok, width), F32), v((tok, width), F32), v((width, tok), BF), v((width, tok), BF),
         v((keys, 2 * width), BF), v((2 * width, keys), BF), v((16, tok), F32), v((width, tok), BF), v((tok, width), F32),
         v((full, tok), F32), v((keys, tok), F32), v((full, 128), F32), v((keys, 128), F32), v((tok, width), BF),
-        v((width, 6 * width), BF), v((8, 6 * width), F32), v((8, full), F32),
-        pltpu.SemaphoreType.DMA((32,)), pltpu.SemaphoreType.DMA((3 * seq,)), pltpu.SemaphoreType.DMA((3 * seq,)),
+        v((width, 6 * width), BF), v((8, 6 * width), F32), v((8, full), F32), v((seq, tok, width), BF),
+        pltpu.SemaphoreType.DMA((32,)), pltpu.SemaphoreType.DMA((16,)), pltpu.SemaphoreType.DMA((16,)),
     ]
     outs = pl.pallas_call(
         functools.partial(forward_kernel, dims, args[4].shape[1]),
@@ -609,7 +638,22 @@
     loads = Bag()
     loads["x2"] = local.start(r.in_x2, r.x2)
     loads["cot"] = local.start(r.in_cot, r.cot)
-    for n in K2_WEIGHTS:
+    load_base = local.used
+    local.used += 2 * seq
+
+    def load_chunk(n, c):
+        if n:
+            ca, cb = (c // 2, c % 2) if isinstance(c, int) else (lax.div(c, 2), lax.rem(c, 2))
+            src, dst = r.w_fc2.at[ca, cb], r.g_fc2.at[ca, cb]
+        else:
+            cols = pl.ds(c * chunk if isinstance(c, int) else pl.multiple_of(c * chunk, chunk), chunk)
+            src, dst = r.w_fc1.at[:, :, :, :, cols], r.g_fc1.at[:, :, :, :, cols]
+        return pltpu.make_async_copy(src, dst, r.lsem.at[load_base + 2 * c + n])
+
+    for c in range(seq):
+        for n in range(2):
+            load_chunk(n, c).start()
+    for n in K2_WEIGHTS[2:]:
         loads["w_" + n] = local.start(r["w_" + n], r["g_" + n])
     for n in K2_LOADS[1:]:
         loads[n] = local.start(r["in_" + n], r[n])
@@ -714,6 +758,13 @@
     def weight(n):
         return r["g_" + n][...].reshape(width, width)
 
+    core_base = remote.slots(seq)
+
+    def core_copy(c):
+        ca, cb = (c // 2, c % 2) if isinstance(c, int) else (lax.div(c, 2), lax.rem(c, 2))
+        peer = d + (1 - 2 * bits[0]) * stride
+        return remote.make(r.g_fc2.at[ca, cb, 1 - bits[0]], r.r_fc20.at[ca, cb], core_base + c, {DP: peer})
+
     v = pltpu.VMEM
     dkv_copies = []
     quarter = 2 * width // seq
@@ -774,12 +825,12 @@
             dm_ref[...] = (pick(mods, seg, 5, width) * r.cot[...].astype(F32)).astype(BF)
             m_ref[...] = jnp.zeros_like(m_ref)
             dh_ref[...] = jnp.zeros_like(dh_ref)
-            loads.w_fc1.wait()
-            loads.w_fc2.wait()
             g1, g2 = r.g_fc1, r.g_fc2
             k0, k1 = math.sqrt(2.0 / math.pi), 0.044715
 
             def one(c, carry):
+                load_chunk(0, c).wait()
+                load_chunk(1, c).wait()
                 cols = pl.ds(pl.multiple_of(c * chunk, chunk), chunk)
                 ca, cb = lax.div(c, 2), lax.rem(c, 2)
                 w1 = g1[:, :, :, :, cols].reshape(width, chunk)
@@ -800,10 +851,13 @@
                         lane = (q % 2) * 2 * group
                         g2[ca, cb, g0, q // 2, :, lane : lane + group] = val[:half, q * group : (q + 1) * group]
                         g2[ca, cb, g0, q // 2, :, lane + group : lane + 2 * group] = val[half:, q * group : (q + 1) * group]
+                core_copy(c).start()
                 return carry
 
             lax.fori_loop(0, seq, one, 0)
-            grads.fc2.begin()
+            grads.fc2.copies = [functools.partial(core_copy, c) for c in range(seq)]
+            for c in range(seq):
+                remote.open.append(lambda c=c: core_copy(c).wait_send())
             grads.fc1.begin()
             dy = r.cot[...].astype(F32)
             m = m_ref[...]
@@ -816,6 +870,7 @@
             clip_sum(3, dh)
             clip_sum(4, dh * nw)
             r.dx[...] = dy + norm_back(dh * (1.0 + pick(mods, seg, 4, width)), nw, rstd)
+            grads.fc2.step()
 
         pl.run_scoped(feed, v((tok, width), BF), v((width, tok), BF), v((tok, width), BF), v((tok, width), F32), v((tok, width), F32))
 
@@ -829,7 +884,7 @@
             grads.cout.begin()
             tcol = column(codes[2:3, :keys])
             biasc[...] = jnp.where(jnp.broadcast_to(tcol[:, :1], (keys, tok)) == seg_row, 0.0, MASKED)
-            grads.fc2.step()
+            grads.fc1.step()
             kv = r.kv
 
             def pair(p, carry):
@@ -852,10 +907,8 @@
                 kv[:, vcols] = jnp.concatenate(parts_v, axis=1).astype(BF)
                 return carry
 
-            lax.fori_loop(0, 2, pair, 0)
-            grads.fc1.step()
-            lax.fori_loop(2, H // 2, pair, 0)
-            begin_kv()
+            lax.fori_loop(0, H // 2, pair, 0)
+            grads.fc2.step()
             dcq = dcqT[...].T.astype(BF)
             loads.w_cq.wait()
             loads.h2T.wait()
@@ -867,6 +920,7 @@
 
         pl.run_scoped(cross_back, v((width, tok), BF), v((width, tok), F32), v((keys, tok), F32))
 
+        grads.fc1.step()
         for c in (loads.w_proj, loads.aout, loads.oT):
             c.wait()
         dx1 = r.dx[...]
@@ -878,11 +932,11 @@
             send_do(k).start()
         r.dorecv[s] = r.dosend[s]
         grads.cq.begin()
+        grads.cout.step()
+        begin_kv()
         clip_sum(2, dx1 * r.aout[...])
         square("proj", lambda i: r.oT[i], da)
         grads.proj.begin()
-        grads.fc2.step()
-        grads.fc1.step()
         for c in (loads.qT, loads.kT, loads.kn, loads.vn, loads.lse):
             c.wait()
 
@@ -916,7 +970,8 @@
                 return carry
 
             lax.fori_loop(0, 2, block, 0)
-            step_kv()
+            grads.fc1.step()
+            grads.fc2.step()
             lax.fori_loop(2, seq, block, 0)
             for h in range(hl):
                 for b in range(seq):
@@ -943,10 +998,9 @@
 
     for k in range(1, seq):
         send_dq(k).start()
-    for n in ("cout", "cq", "proj"):
+    step_kv()
+    for n in ("cq", "proj", "cout"):
         grads[n].step()
-    grads.fc2.step()
-    grads.fc1.step()
     r.dqr[s] = r.dqs[s]
 
     def tail(h1, text, wqkv, wckv, dqf):
@@ -959,21 +1013,8 @@
         gq = tn(h1[...].reshape(full, width), r.dqs[...].reshape(full, 3 * group))
         r.g_qkv[...] = gq.astype(BF).reshape(2, 2, 2, width // BLOCKS, 3 * group)
         grads.qkv.begin()
-        end_kv()
-        kv_base = remote.slots(seq)
-
-        def send_kv(k):
-            to = lax.rem(s + k, seq)
-            return remote.make(r.dkvq.at[to], r.dkvl.at[s], kv_base + k, {SEQ: to})
-
-        for k in range(1, seq):
-            send_kv(k).start()
-        r.dkvl[s] = r.dkvq[s]
-        tail_loads[2].wait()
-        gc = tn(text[...].reshape(keys, dc_all), r.dkvq[...].reshape(keys, quarter))
-        r.g_ckv[...] = gc.astype(BF).reshape(2, 2, 2, dc_all // BLOCKS, quarter)
-        grads.ckv.begin()
         grads.qkv.step()
+        grads.fc2.step()
         for k in range(1, seq):
             send_dq(k).wait_recv()
         for b in range(seq):
@@ -998,12 +1039,22 @@
         back = norm_back(dh1 * (1.0 + pick(mods, seg, 1, width)), nx, rstd)
         r.out_grad_frames[...] = (r.dx[...] + back).astype(BF)
         store("grad_frames")
-        grads.fc1.step()
-        grads.ckv.step()
-        grads.qkv.step()
-        for n in ("cout", "cq", "proj"):
+        end_kv()
+        kv_base = remote.slots(seq)
+
+        def send_kv(k):
+            to = lax.rem(s + k, seq)
+            return remote.make(r.dkvq.at[to], r.dkvl.at[s], kv_base + k, {SEQ: to})
+
+        for k in range(1, seq):
+            send_kv(k).start()
+        r.dkvl[s] = r.dkvq[s]
+        tail_loads[2].wait()
+        gc = tn(text[...].reshape(keys, dc_all), r.dkvq[...].reshape(keys, quarter))
+        r.g_ckv[...] = gc.astype(BF).reshape(2, 2, 2, dc_all // BLOCKS, quarter)
+        grads.ckv.begin()
+        for n in ("qkv", "cq", "proj", "cout", "fc1", "ckv"):
             grads[n].step()
-        grads.fc2.step()
         for c in dm_copies:
             c().wait_recv()
         total = r.dmod[:, pl.ds(pl.multiple_of(s * part, part), part)]
@@ -1020,14 +1071,7 @@
             return carry
 
         lax.fori_loop(1, dp, start_dm, 0)
-        for k in range(1, seq):
-            send_kv(k).wait_recv()
-        tail_loads[3].wait()
-        gt = nt(r.dkvl[0], wckv[:, 0:quarter])
-        for b in range(1, seq):
-            gt = gt + nt(r.dkvl[b], wckv[:, b * quarter : (b + 1) * quarter])
-        r.out_grad_text[...] = gt.astype(BF)
-        store("grad_text")
+        grads.fc2.step()
         grads.qkv.step()
         q_base = remote.slots(3)
 
@@ -1055,7 +1099,17 @@
             def _():
                 r.rq[slot] = r.fq[t]
 
-        for n in ("cout", "cq", "proj", "ckv", "fc2", "cout", "cq", "proj", "ckv", "fc1", "cout", "cq", "proj"):
+        for n in ("cout", "cq", "proj", "ckv"):
+            grads[n].step()
+        for k in range(1, seq):
+            send_kv(k).wait_recv()
+        tail_loads[3].wait()
+        gt = nt(r.dkvl[0], wckv[:, 0:quarter])
+        for b in range(1, seq):
+            gt = gt + nt(r.dkvl[b], wckv[:, b * quarter : (b + 1) * quarter])
+        r.out_grad_text[...] = gt.astype(BF)
+        store("grad_text")
+        for n in ("cq", "proj", "cout", "ckv", "fc1", "cq", "proj"):
             grads[n].step()
 
         def wait_dm(j, carry):

time: 185 us -> 169 us (0.914)
  Pallas kernels: 181 us -> 166 us
    pallas_call x1, Pallas kernels: 123 us -> 114 us  [run_backward(): pl.pallas_call(functools.partial(backward_kernel, dims, tuple(names), dp)...]
    pallas_call x1, Pallas kernels: 55.4 us -> 49.2 us  [run_forward(): pl.pallas_call(functools.partial(forward_kernel, dims, args[4].shape[1]),...]
where the time goes in v4:
time: 169 us
  Pallas kernels  166 us (98%)
    pallas_call x1, Pallas kernels, run_backward(): pl.pallas_call(functools.partial(backward_kernel, dims, tuple(names), dp)...  114 us
    pallas_call x1, Pallas kernels, run_forward(): pl.pallas_call(functools.partial(forward_kernel, dims, args[4].shape[1]),...  49.2 us

profile of v4, /device:TPU:0, one launch (start us, length us, event | category | flops | bytes accessed | tf_op | source)
XLA Modules:
  0.0 168.8 jit_solution(10230144443095608812)
XLA Ops:
  0.6 0.7 pad_convert_fusion
  1.3 0.1 multiply_cosine_fusion.1
  1.5 0.6 multiply_convert_fusion.1.refs_5_
  2.1 0.1 multiply_cosine_fusion
  2.3 0.6 pad.9.refs_4_
  2.9 49.2 %forward_part.1 = (bf16[4,256,768]{2,1,0:T(8,128)(2,1)}, bf16[192,1024]{1,0:T(8,128)(2,1)}, bf16[192,1024]{1,0:T(8,128)(2,1)}, bf16[3,1024,64]{2,1,0:T(8,128)(2,...) custom-call(bf16[256,768]{1,0:T(8,128)(2,1)} %bitcast.20, ...), custom_call_target="tpu_custom_call" | custom-call | tf_op jit(solution)/shard_map/forward_part/pallas_call | solution.py:411
  52.0 113.8 %backward_part.1 = (bf16[256,768]{1,0:T(8,128)(2,1)}, bf16[256,768]{1,0:T(8,128)(2,1)}, bf16[192,1024]{1,0:T(8,128)(2,1)}, f32[96,1152]{1,0:T(8,128)}, f32[96,57...) custom-call(f32[8,1024]{1,0:T(8,128)} %get-tuple-element.52.refs_0_,, ...), custom_call_target="tpu_custom_call" | custom-call | tf_op jit(solution)/shard_map/backward_part/pallas_call | solution.py:1260
  165.8 2.8 %hand_over.1 = (bf16[256,768]{1,0:T(8,128)(2,1)}, bf16[256,768]{1,0:T(8,128)(2,1)}, bf16[192,1024]{1,0:T(8,128)(2,1)}, f32[96,1152]{1,0:T(8,128)}, f32[96,576]{1...) custom-call(bf16[256,768]{1,0:T(8,128)(2,1)} %get-tuple-element.71.r, ...), custom_call_target="tpu_custom_call" | custom-call | tf_op jit(solution)/shard_map/hand_over/pallas_call | solution.py:1290
  (3 shorter events, 0.0 us)

commit v5 on v4

--- a/solution.py
+++ b/solution.py
@@ -203,7 +203,8 @@
     load_x.wait()
     load_own.wait()
     load_ada.wait()
-    mods[...] = nn(emb[...], wada[...])
+    mods[...] = jnp.zeros_like(mods)
+    mods[0:segs, :] = nn(emb[...], wada[...])
     save_mods = local.start(mods, outs.mods)
     for c in load_wg:
         c.wait()
@@ -358,7 +359,7 @@
             lsec[pl.ds(2 * p + a, 1), :] = peak + jnp.log(total)
         return carry
 
-    lax.fori_loop(0, H // 2, cross, 0)
+    lax.fori_loop(0, H // 2, cross, 0, unroll=2)
     x2[...] = x1[...] + tn(coT[...], wco[...])
     saves += [local.start(a, b) for a, b in ((lsec, outs.lsec), (coT, outs.coT), (x2, outs.x2))]
     for m in (1, 2):
@@ -1310,9 +1311,11 @@
     keys = segs * tl * seq
     group = (H // seq) * HD
     dims = (seq, tok, full, width, keys, group, dc)
-    emb = embed_steps(jnp.pad(step_ids[0], (0, 8 - segs)), width).astype(BF)
+    emb = embed_steps(step_ids[0], width).astype(BF)
     span = width // dp
-    emb_parts = jnp.pad(jnp.swapaxes(emb.reshape(8, dp, span), 0, 1), ((0, 0), (0, 0), (0, 128 - span)))
+    emb_parts = jnp.pad(
+        jnp.swapaxes(emb.reshape(segs, dp, span), 0, 1), ((0, 0), (0, 8 - segs), (0, 128 - span))
+    )
     x = frames[0]
     text = text_states.reshape(segs * tl, dc)
     fwd = run_forward(dims, (x, text, seg_ids, padding, text_len, emb, w_ada, w_qkv, w_ckv, w_proj, w_cq, w_cout))

time: 169 us -> 169 us (level)
  no operation moved by 1% of the time
where the time goes in v5:
time: 169 us; the launch traced here: 168 us
  Pallas kernels  165 us (98%)
    pallas_call x1, Pallas kernels, run_backward(): pl.pallas_call(functools.partial(backward_kernel, dims, tuple(names), dp)...  114 us
    pallas_call x1, Pallas kernels, run_forward(): pl.pallas_call(functools.partial(forward_kernel, dims, args[4].shape[1]),...  48.8 us

profile of v5, /device:TPU:0, one launch (start us, length us, event | category | flops | bytes accessed | tf_op | source)
XLA Modules:
  0.0 168.4 jit_solution(14656634240506581014)
XLA Ops:
  0.6 0.7 convert_bitcast_fusion
  1.3 0.1 multiply_cosine_fusion.1
  1.5 0.6 fusion.1.refs_5_
  2.1 0.1 multiply_cosine_fusion
  2.2 0.6 pad.4.refs_4_
  2.9 48.8 %forward_part.1 = (bf16[4,256,768]{2,1,0:T(8,128)(2,1)}, bf16[192,1024]{1,0:T(8,128)(2,1)}, bf16[192,1024]{1,0:T(8,128)(2,1)}, bf16[3,1024,64]{2,1,0:T(8,128)(2,...) custom-call(bf16[256,768]{1,0:T(8,128)(2,1)} %bitcast.21, ...), custom_call_target="tpu_custom_call" | custom-call | tf_op jit(solution)/shard_map/forward_part/pallas_call | solution.py:412
  51.6 113.8 %backward_part.1 = (bf16[256,768]{1,0:T(8,128)(2,1)}, bf16[256,768]{1,0:T(8,128)(2,1)}, bf16[192,1024]{1,0:T(8,128)(2,1)}, f32[96,1152]{1,0:T(8,128)}, f32[96,57...) custom-call(f32[8,1024]{1,0:T(8,128)} %get-tuple-element.52.refs_0_,, ...), custom_call_target="tpu_custom_call" | custom-call | tf_op jit(solution)/shard_map/backward_part/pallas_call | solution.py:1261
  165.4 2.8 %hand_over.1 = (bf16[256,768]{1,0:T(8,128)(2,1)}, bf16[256,768]{1,0:T(8,128)(2,1)}, bf16[192,1024]{1,0:T(8,128)(2,1)}, f32[96,1152]{1,0:T(8,128)}, f32[96,576]{1...) custom-call(bf16[256,768]{1,0:T(8,128)(2,1)} %get-tuple-element.71.r, ...), custom_call_target="tpu_custom_call" | custom-call | tf_op jit(solution)/shard_map/hand_over/pallas_call | solution.py:1291
  (3 shorter events, 0.0 us)
